TPU v7x, 32 devices: a whole 2x2x4 slice. The times are simulated.
32 devices in a mesh: rect: 4 (over y, x), slab: 8 (over z, core).
Axes of the slice: x: 2, y: 2, z: 4, core: 2. Of those that a mesh axis runs over, the one named last changes fastest.
Arguments:
- modes_now: bfloat16 [4, 512, 256, 256], P('rect', None, 'slab'), may hold values from -4 to 4
- modes_prev: bfloat16 [4, 512, 256, 256], P('rect', None, 'slab'), may hold values from -4 to 4
- face_partner: int32 [4], replicated, may hold values from 0 to 3, each once
Outputs:
- modes_next: bfloat16 [4, 512, 256, 256], P('rect', None, 'slab')
- interface_force: float32 [4, 6, 512, 256], P('rect', None, 'slab')
Inputs may be any that keep to these rules, and one draw needn't show every extreme that they name: `face_partner`: A permutation of the large rectangles; a rectangle may abut itself.
All inputs are finite; a program needn't handle non-finite values.
Results may differ from a plain program's by a relative error of at most 0.0048.
The roundings to bfloat16 on the way count: a program that leaves them out, or rounds other values in their place, can miss the bound.
Values may be sent and summed in bfloat16 or wider, within the bound.
No kernel may reach another device: no remote copies, remote signals or barrier semaphores. Data moves between devices by JAX's collectives and lax.ppermute only.
A program may use at most 64 MiB of HBM per device.

v0:
```python
import functools
import math

import jax
import jax.numpy as jnp
import ml_dtypes
import numpy as np
from jax import lax
from jax.experimental import pallas as pl
from jax.experimental.pallas import tpu as pltpu
from jax.sharding import PartitionSpec as P

courant_sq = 1.0 / 3.0
coeffs = (1.5, -0.15, 2.0 / 180.0)
bf16 = ml_dtypes.bfloat16
PLANES = 6
LANES = 128
GROUP = 16
USED = PLANES * GROUP


def cosine_table(length):
    mode_index = np.arange(length, dtype=np.int64)[:, None]
    cell_index = np.arange(length, dtype=np.int64)[None, :]
    phase = mode_index * (2 * cell_index + 1) % (4 * length)
    angles = phase.astype(np.float32) * np.float32(math.pi / (2.0 * length))
    weights = np.where(mode_index == 0, math.sqrt(1.0 / length), math.sqrt(2.0 / length))
    return weights.astype(np.float32) * np.cos(angles)


def plane_columns(depth_z):
    table = cosine_table(depth_z)
    return np.concatenate([table[:, :3], table[:, depth_z - 3 :]], axis=1).astype(bf16)


def spread_columns(depth_z):
    columns = plane_columns(depth_z)
    out = np.zeros((depth_z, LANES), bf16)
    out[:, :USED] = np.repeat(columns, GROUP, axis=1)
    return out


def force_matrix():
    own = np.zeros((PLANES, PLANES), np.float64)
    other = np.zeros((PLANES, PLANES), np.float64)
    for m in range(3):
        for k in range(3 - m):
            weight = courant_sq * coeffs[m + k]
            other[5 - k, m] += weight
            own[k, m] -= weight
            other[k, 5 - m] += weight
            own[5 - k, 5 - m] -= weight
    full = np.zeros((2 * LANES, LANES), np.float64)
    for row in range(GROUP):
        full[row:USED:GROUP, row:USED:GROUP] = own
        full[LANES + row : LANES + USED : GROUP, row:USED:GROUP] = other
    terms = []
    rest = full
    for _ in range(3):
        term = rest.astype(np.float32).astype(bf16)
        terms.append(term)
        rest = rest - term.astype(np.float64)
    return np.concatenate(terms, axis=0)


def gain_polynomial(degree):
    top = math.pi * math.pi

    def exact(t):
        t = np.asarray(t, np.float64)
        theta = np.sqrt(np.maximum(t, 1e-12))
        return np.where(t > 1e-10, (2.0 * np.sin(0.5 * theta) / theta) ** 2, 1.0)

    fit = np.polynomial.chebyshev.Chebyshev.interpolate(exact, degree, domain=[0.0, top * 1.0001])
    return [float(c) for c in fit.convert(kind=np.polynomial.Polynomial, domain=[-1, 1]).coef]


def row_mask():
    rows = lax.broadcasted_iota(jnp.int32, (GROUP, LANES), 0)
    lanes = lax.broadcasted_iota(jnp.int32, (GROUP, LANES), 1)
    return (lanes % GROUP == rows) & (lanes < USED)


def packed_lower_mask(shape):
    lanes = lax.broadcasted_iota(jnp.int32, shape, len(shape) - 1)
    tile = lanes // LANES
    inner = lanes % LANES
    plane = jnp.where(inner < USED, inner // GROUP, 2 * tile + (inner - USED) // GROUP)
    return plane < 3


def sections_kernel(now_ref, columns_ref, z_ref, *pack_refs):
    rows = now_ref.shape[0]
    count = len(pack_refs)
    group_x = rows // 4
    mask = row_mask()[None]
    lane = lax.broadcasted_iota(jnp.int32, (group_x, LANES), 1)
    halves = [[] for _ in pack_refs]
    for part in range(4):
        block = now_ref[part * group_x : (part + 1) * group_x]
        flat = block.reshape(group_x * block.shape[1], block.shape[2])
        section = jnp.dot(flat, columns_ref[...], preferred_element_type=jnp.float32)
        section = section.reshape(group_x, count, GROUP, LANES)
        for half in range(count):
            picked = jnp.sum(jnp.where(mask, section[:, half], 0.0), axis=1)
            picked = picked.astype(jnp.bfloat16)
            z_ref[part * group_x : (part + 1) * group_x, half * LANES : (half + 1) * LANES] = picked
            halves[half].append(picked.astype(jnp.float32))
    for half, pack_ref in enumerate(pack_refs):
        for tile in range(3):
            moved = pltpu.roll(halves[half][3], USED - 32 * tile, 1)
            pack_ref[:, tile * LANES : (tile + 1) * LANES] = jnp.where(
                lane < USED, halves[half][tile], moved
            ).astype(jnp.bfloat16)


def neighbours(face_ref, rect):
    partner = face_ref[rect]
    source = jnp.int32(0)
    for index in range(face_ref.shape[0]):
        source = source + jnp.where(face_ref[index] == rect, jnp.int32(index), jnp.int32(0))
    return partner, source


def forward_kernel(face_ref, place_ref, pack_a_ref, pack_b_ref, got_a_ref, got_b_ref, send_a_ref, send_b_ref):
    rect = place_ref[0]
    lower = packed_lower_mask(pack_a_ref.shape)
    for step, pack_ref, got_ref, send_ref in (
        (2, pack_a_ref, got_a_ref, send_a_ref),
        (1, pack_b_ref, got_b_ref, send_b_ref),
    ):
        partner, source = neighbours(face_ref, rect ^ step)
        own = pack_ref[...].astype(jnp.float32)
        got = got_ref[...].astype(jnp.float32)
        for_lower = jnp.where(partner == rect, own, got)
        for_upper = jnp.where(source == rect, own, got)
        send_ref[...] = jnp.where(lower, for_lower, for_upper).astype(jnp.bfloat16)


def pick(code, first, second, third):
    return jnp.where(code == 0, first, jnp.where(code == 1, second, third))


def forces_kernel(routed, face_ref, place_ref, z_ref, *refs):
    own_refs, one_refs, two_refs = [refs[i : len(refs) - 3 : 3] for i in range(3)]
    table_ref, near_ref, piece_ref = refs[-3:]
    count = len(own_refs)
    rect = place_ref[0]
    partner, source = neighbours(face_ref, rect)
    packed_rows = own_refs[0].shape[0]
    lower = packed_lower_mask(own_refs[0].shape)
    blocks = packed_rows // GROUP
    lane = lax.broadcasted_iota(jnp.int32, (blocks, GROUP, LANES), 2)
    for half, (own_ref, one_ref, two_ref) in enumerate(zip(own_refs, one_refs, two_refs)):
        if routed:
            step = half + 1
            code_lower = jnp.where(partner == rect, 0, jnp.where(partner == (rect ^ step), 1, 2))
            code_upper = jnp.where(source == rect, 0, jnp.where(source == (rect ^ step), 1, 2))
        else:
            code_lower, code_upper = jnp.int32(1), jnp.int32(2)
        values = [ref[...].astype(jnp.float32) for ref in (own_ref, one_ref, two_ref)]
        packed = jnp.where(lower, pick(code_lower, *values), pick(code_upper, *values))
        tiles = [
            packed[:, tile * LANES : (tile + 1) * LANES].reshape(blocks, GROUP, LANES) for tile in range(3)
        ]
        moved = [
            pltpu.roll(packed[:, tile * LANES : (tile + 1) * LANES], 32 * (tile + 1), 1).reshape(
                blocks, GROUP, LANES
            )
            for tile in range(3)
        ]
        last = jnp.where(lane < 32, moved[0], jnp.where(lane < 64, moved[1], moved[2]))
        for group, value in enumerate(tiles + [last]):
            value = jnp.where(lane < USED, value, 0.0).astype(jnp.bfloat16)
            for block in range(blocks):
                start = (block * 4 + group) * GROUP
                near_ref[start : start + GROUP, half * LANES : (half + 1) * LANES] = value[block]
    table = table_ref[...]

    def transform(ref, half):
        modes = ref[:, half * LANES : half * LANES + USED]
        out = lax.dot_general(modes, table, (((0,), (0,)), ((), ())), preferred_element_type=jnp.float32)
        out = out.astype(jnp.bfloat16).astype(jnp.float32)
        return [out[plane * GROUP : (plane + 1) * GROUP] for plane in range(PLANES)]

    for half in range(count):
        own = transform(z_ref, half)
        near = transform(near_ref, half)
        jump_up = [near[k] - own[5 - k] for k in range(3)]
        jump_down = [near[5 - k] - own[k] for k in range(3)]
        force = [None] * PLANES
        for m in range(3):
            down = coeffs[m] * jump_down[0]
            up = coeffs[m] * jump_up[0]
            for k in range(1, 3 - m):
                down = down + coeffs[m + k] * jump_down[k]
                up = up + coeffs[m + k] * jump_up[k]
            force[m] = courant_sq * down
            force[5 - m] = courant_sq * up
        width = piece_ref.shape[2] // PLANES
        for slot in range(piece_ref.shape[0]):
            parts = [plane[:, slot * width : (slot + 1) * width] for plane in force]
            piece_ref[slot, half * GROUP : (half + 1) * GROUP, :] = jnp.concatenate(parts, axis=1).astype(
                jnp.bfloat16
            )


def update_kernel(poly, sides, place_ref, now_ref, prev_ref, z_ref, near_ref, mix_ref, planes_ref, out_ref, force_ref):
    rows, local_y, depth_z = now_ref.shape
    step = pl.program_id(0)
    slab = place_ref[1]
    mask = row_mask()[None]
    for half in range(local_y // GROUP):
        cols = slice(half * LANES, (half + 1) * LANES)
        both = jnp.concatenate([z_ref[:, cols], near_ref[:, cols]], axis=1)
        modes = jnp.dot(
            jnp.concatenate([both, both, both], axis=1), mix_ref[...], preferred_element_type=jnp.float32
        )
        spread = jnp.where(mask, jnp.broadcast_to(modes[:, None, :], (rows, GROUP, LANES)), 0.0)
        spread = spread.astype(jnp.bfloat16).reshape(rows * GROUP, LANES)
        force = jnp.dot(spread, planes_ref[...], preferred_element_type=jnp.float32)
        force_ref[:, half * GROUP : (half + 1) * GROUP, :] = force.reshape(rows, GROUP, depth_z)
    scale = math.pi * math.pi / 3.0
    y_index = lax.broadcasted_iota(jnp.int32, (local_y, depth_z), 0) + slab * local_y
    z_index = lax.broadcasted_iota(jnp.int32, (local_y, depth_z), 1)
    y_part = y_index.astype(jnp.float32) / sides[1]
    z_part = z_index.astype(jnp.float32) / sides[2]
    base = scale * (y_part * y_part + z_part * z_part)

    def body(row, carry):
        x_index = jnp.full((1, 1), step * rows + row, jnp.int32)
        x_part = x_index.astype(jnp.float32) / sides[0]
        theta_sq = base + scale * (x_part * x_part)
        gain = poly[-1] * theta_sq + poly[-2]
        for coefficient in poly[-3::-1]:
            gain = gain * theta_sq + coefficient
        two_cos = 2.0 - theta_sq * gain
        value = two_cos * now_ref[row].astype(jnp.float32) - prev_ref[row].astype(jnp.float32)
        out_ref[row] = (value + gain * force_ref[row]).astype(jnp.bfloat16)
        return carry

    lax.fori_loop(0, rows, body, 0, unroll=2)


def planes_kernel(arrived_ref, table_ref, out_ref):
    out = lax.dot_general(
        arrived_ref[...], table_ref[...], (((0,), (0,)), ((), ())), preferred_element_type=jnp.float32
    )
    out_ref[...] = out


def smem():
    return pl.BlockSpec(memory_space=pltpu.SMEM)


def shards(modes_now, modes_prev, face_partner):
    slab_count = lax.axis_size("slab")
    rect_count = lax.axis_size("rect")
    slab_rank = lax.axis_index("slab")
    rect_rank = lax.axis_index("rect")
    _, length_x, local_y, depth_z = modes_now.shape
    length_y = local_y * slab_count
    local_x = length_x // slab_count
    assert local_y % GROUP == 0 and length_x % (4 * GROUP) == 0
    count = local_y // GROUP
    bf = jnp.bfloat16
    place = jnp.stack([rect_rank, slab_rank]).astype(jnp.int32)
    current = modes_now[0]
    earlier = modes_prev[0]
    columns = jnp.asarray(spread_columns(depth_z))
    planes = jnp.asarray(np.ascontiguousarray(spread_columns(depth_z).T))
    mix = jnp.asarray(force_matrix())
    table_x = jnp.asarray(cosine_table(length_x).astype(bf16))
    table_y = jnp.asarray(cosine_table(length_y).astype(bf16))

    block_x = 4 * GROUP
    packed = jax.ShapeDtypeStruct((length_x // 4, 3 * LANES), bf)
    z_own, *packs = pl.pallas_call(
        sections_kernel,
        grid=(length_x // block_x,),
        in_specs=[
            pl.BlockSpec((block_x, local_y, depth_z), lambda i: (i, 0, 0)),
            pl.BlockSpec((depth_z, LANES), lambda i: (0, 0)),
        ],
        out_specs=[
            pl.BlockSpec((block_x, count * LANES), lambda i: (i, 0)),
            *[pl.BlockSpec((GROUP, 3 * LANES), lambda i: (i, 0)) for _ in range(count)],
        ],
        out_shape=[jax.ShapeDtypeStruct((length_x, count * LANES), bf)] + [packed] * count,
        name="sections",
    )(current, columns)

    routed = rect_count == 4 and count == 2
    if routed:

        def hop(value, step):
            return lax.ppermute(value, "rect", [(j, j ^ step) for j in range(rect_count)])

        ones = [hop(packs[0], 1), hop(packs[1], 2)]
        sends = pl.pallas_call(
            forward_kernel,
            in_specs=[smem(), smem()] + [pl.BlockSpec() for _ in range(4)],
            out_shape=[packed, packed],
            name="forward",
        )(face_partner, place, *packs, *ones)
        twos = [hop(sends[0], 2), hop(sends[1], 1)]
    else:
        rect_ids = jnp.arange(rect_count, dtype=jnp.int32)
        partner = jnp.sum(jnp.where(rect_ids == rect_rank, face_partner, 0))
        source = jnp.sum(jnp.where(face_partner == rect_rank, rect_ids, 0))
        every = [lax.all_gather(pack, "rect", axis=0) for pack in packs]
        ones = [lax.dynamic_index_in_dim(value, partner, 0, keepdims=False) for value in every]
        twos = [lax.dynamic_index_in_dim(value, source, 0, keepdims=False) for value in every]
    routes = [value for triple in zip(packs, ones, twos) for value in triple]

    near, pieces = pl.pallas_call(
        functools.partial(forces_kernel, routed),
        in_specs=[smem(), smem()] + [pl.BlockSpec() for _ in range(2 + len(routes))],
        out_shape=[
            jax.ShapeDtypeStruct((length_x, count * LANES), bf),
            jax.ShapeDtypeStruct((slab_count, local_y, PLANES * local_x), bf),
        ],
        name="forces",
    )(face_partner, place, z_own, *routes, table_x)

    arrived = lax.all_to_all(pieces, "slab", split_axis=0, concat_axis=0, tiled=True)

    rows = 32
    fresh = pl.pallas_call(
        functools.partial(update_kernel, gain_polynomial(6), (length_x, length_y, depth_z)),
        grid=(length_x // rows,),
        in_specs=[
            smem(),
            pl.BlockSpec((rows, local_y, depth_z), lambda i: (i, 0, 0)),
            pl.BlockSpec((rows, local_y, depth_z), lambda i: (i, 0, 0)),
            pl.BlockSpec((rows, count * LANES), lambda i: (i, 0)),
            pl.BlockSpec((rows, count * LANES), lambda i: (i, 0)),
            pl.BlockSpec(mix.shape, lambda i: (0, 0)),
            pl.BlockSpec(planes.shape, lambda i: (0, 0)),
        ],
        out_specs=pl.BlockSpec((rows, local_y, depth_z), lambda i: (i, 0, 0)),
        out_shape=jax.ShapeDtypeStruct((length_x, local_y, depth_z), bf),
        scratch_shapes=[pltpu.VMEM((rows, local_y, depth_z), jnp.float32)],
        name="update",
    )(place, current, earlier, z_own, near, mix, planes)

    forcing = pl.pallas_call(
        planes_kernel,
        out_shape=jax.ShapeDtypeStruct((PLANES * local_x, length_y), jnp.float32),
        name="planes",
    )(arrived.reshape(length_y, PLANES * local_x), table_y)
    return (fresh[None], forcing.reshape(1, PLANES, local_x, length_y))


def solution(mesh):
    return jax.shard_map(
        shards,
        mesh=mesh,
        in_specs=(P("rect", None, "slab", None), P("rect", None, "slab", None), P()),
        out_specs=(P("rect", None, "slab", None), P("rect", None, "slab", None)),
        check_vma=False,
    )
```

profile of v0, /device:TPU:1, one launch (start us, length us, event | category | flops | bytes accessed | tf_op | source)
XLA Modules:
  0.0 61.9 jit_solution(972116314967332463)
XLA Ops:
  0.6 8.4 %sections.1 = (bf16[512,256]{1,0:T(8,128)(2,1)}, bf16[128,384]{1,0:T(8,128)(2,1)}, bf16[128,384]{1,0:T(8,128)(2,1)}) custom-call(bf16[512,32,256]{2,1,0:T(8,128)(2,1)} %bitcast.7, bf16[256,128]{1,0:T(8,128)(2,1)} %constant.18.clone.columns_ref), custom_call_target="tpu_custom_call" | custom-call | tf_op jit(solution)/shard_map/sections/pallas_call | solution.py:278
  9.1 2.0 %collective-permute-start = (bf16[128,384]{1,0:T(8,128)(2,1)}, bf16[128,384]{1,0:T(8,128)(2,1)S(1)}, u32[]{:S(2)}, u32[]{:S(2)}) collective-permute-start(bf16[128,384]{1,0:T(8,128)(2,1)} %get-tuple-element.10.pack_a_ref.refs_0_), channel_id=1, source_target_pairs={{0,8},{8,0},{16,24},{24,16},{1,9},{9,1},{17,25},{25,17},{2,10},{10... | collective-permute-start | bytes 294920 | tf_op jit(solution)/shard_map/ppermute | solution.py:297
  11.1 1.2 %collective-permute-start.1 = (bf16[128,384]{1,0:T(8,128)(2,1)}, bf16[128,384]{1,0:T(8,128)(2,1)S(1)}, u32[]{:S(2)}, u32[]{:S(2)}) collective-permute-start(bf16[128,384]{1,0:T(8,128)(2,1)} %get-tuple-element.11.pack_b_ref.refs_3_), channel_id=1, source_target_pairs={{0,16},{8,24},{16,0},{24,8},{1,17},{9,25},{17,1},{25,9},{2,18},{10... | collective-permute-start | bytes 294920 | tf_op jit(solution)/shard_map/ppermute | solution.py:297
  12.4 0.6 %pad_add_fusion.place_ref = s32[2]{0:T(128)} fusion(s32[1]{0:T(128)} %bitcast.1, s32[1]{0:T(128)} %bitcast), kind=kLoop, calls=%fused_computation | loop fusion | flops 2 | bytes 16 | tf_op jit(solution)/shard_map/stack | solution.py:267
  13.0 0.8 %collective-permute-done.got_a_ref.refs_1_ = bf16[128,384]{1,0:T(8,128)(2,1)S(1)} collective-permute-done((bf16[128,384]{1,0:T(8,128)(2,1)}, bf16[128,384]{1,0:T(8,128)(2,1)S(1)}, u32[]{:S(2)}, u32[]{:S(2)}) %collective-permute-start) | collective-permute-done | bytes 98336 | tf_op jit(solution)/shard_map/ppermute | solution.py:297
  13.9 0.0 copy-start.1
  13.9 0.9 %collective-permute-done.1.got_b_ref.refs_4_ = bf16[128,384]{1,0:T(8,128)(2,1)S(1)} collective-permute-done((bf16[128,384]{1,0:T(8,128)(2,1)}, bf16[128,384]{1,0:T(8,128)(2,1)S(1)}, u32[]{:S(2)}, u32[]{:S(2)}) %collective-permute-start.1) | collective-permute-done | bytes 98336 | tf_op jit(solution)/shard_map/ppermute | solution.py:297
  14.8 0.0 copy-done.1
  14.8 0.0 copy-start.2
  14.8 0.6 %copy-done.2 = bf16[128,384]{1,0:T(8,128)(2,1)} copy-done((bf16[128,384]{1,0:T(8,128)(2,1)}, bf16[128,384]{1,0:T(8,128)(2,1)S(1)}, u32[]{:S(2)}) %copy-start.2) | copy-done | bytes 98328
  15.4 1.8 %forward.1 = (bf16[128,384]{1,0:T(8,128)(2,1)}, bf16[128,384]{1,0:T(8,128)(2,1)}) custom-call(s32[4]{0:T(128)} %face_ref.3, s32[2]{0:T(128)} %pad_add_fusion.place_ref, bf16[128,384]{1,0:T(8,128)(2,1)} %get-tuple-element.10.pack_a_ref.refs_0_, bf16[128,384]{1,0:T(8,128)(2,1)} %get-tuple-element.11.pack_b_ref.refs_3_, bf16[128,384]{1,0:T(8,128)(2,1)} %copy-done.1, ...), custom_call_target="tpu_custom_call" | custom-call | tf_op jit(solution)/shard_map/forward/pallas_call | solution.py:300
  17.2 1.5 %collective-permute-start.2 = (bf16[128,384]{1,0:T(8,128)(2,1)}, bf16[128,384]{1,0:T(8,128)(2,1)S(1)}, u32[]{:S(2)}, u32[]{:S(2)}) collective-permute-start(bf16[128,384]{1,0:T(8,128)(2,1)} %get-tuple-element.12), channel_id=1, source_target_pairs={{0,16},{8,24},{16,0},{24,8},{1,17},{9,25},{17,1},{25,9},{2,18},{10... | collective-permute-start | bytes 294920 | tf_op jit(solution)/shard_map/ppermute | solution.py:297
  18.7 0.4 collective-permute-start.3
  19.1 1.8 %collective-permute-done.2.refs_2_ = bf16[128,384]{1,0:T(8,128)(2,1)S(1)} collective-permute-done((bf16[128,384]{1,0:T(8,128)(2,1)}, bf16[128,384]{1,0:T(8,128)(2,1)S(1)}, u32[]{:S(2)}, u32[]{:S(2)}) %collective-permute-start.2) | collective-permute-done | bytes 98336 | tf_op jit(solution)/shard_map/ppermute | solution.py:297
  20.9 0.0 copy-start.3
  20.9 1.5 %collective-permute-done.3.refs_5_ = bf16[128,384]{1,0:T(8,128)(2,1)S(1)} collective-permute-done((bf16[128,384]{1,0:T(8,128)(2,1)}, bf16[128,384]{1,0:T(8,128)(2,1)S(1)}, u32[]{:S(2)}, u32[]{:S(2)}) %collective-permute-start.3) | collective-permute-done | bytes 98336 | tf_op jit(solution)/shard_map/ppermute | solution.py:297
  22.3 0.0 copy-start.4
  22.3 0.0 copy-done.3
  22.3 0.6 %copy-done.4 = bf16[128,384]{1,0:T(8,128)(2,1)} copy-done((bf16[128,384]{1,0:T(8,128)(2,1)}, bf16[128,384]{1,0:T(8,128)(2,1)S(1)}, u32[]{:S(2)}) %copy-start.4) | copy-done | bytes 98328
  23.0 2.8 %forces.1 = (bf16[512,256]{1,0:T(8,128)(2,1)}, bf16[8,32,384]{2,1,0:T(8,128)(2,1)}) custom-call(s32[4]{0:T(128)} %face_ref.3, s32[2]{0:T(128)} %pad_add_fusion.place_ref, bf16[512,256]{1,0:T(8,128)(2,1)} %get-tuple-element.9.z_ref, bf16[128,384]{1,0:T(8,128)(2,1)} %get-tuple-element.10.pack_a_ref.refs_0_, bf16[128,384]{1,0:T(8,128)(2,1)} %copy-done.1, ...), custom_call_target="tpu_custom_call" | custom-call | tf_op jit(solution)/shard_map/forces/pallas_call | solution.py:316
  25.8 8.2 %all-to-all-start = ((bf16[8,32,384]{2,1,0:T(8,128)(2,1)}), bf16[8,32,384]{2,1,0:T(8,128)(2,1)S(1)}, u32[]{:S(2)}, u32[]{:S(2)}) async-start(bf16[8,32,384]{2,1,0:T(8,128)(2,1)} %get-tuple-element.15), calls=%async_computation | async-start | bytes 393216 | tf_op jit(solution)/shard_map/all_to_all | solution.py:326
  33.9 25.3 %update.1 = bf16[512,32,256]{2,1,0:T(8,128)(2,1)} custom-call(s32[2]{0:T(128)} %pad_add_fusion.place_ref, bf16[512,32,256]{2,1,0:T(8,128)(2,1)} %bitcast.8, bf16[512,32,256]{2,1,0:T(8,128)(2,1)} %bitcast.9, bf16[512,256]{1,0:T(8,128)(2,1)} %get-tuple-element.9.z_ref, bf16[512,256]{1,0:T(8,128)(2,1)} %get-tuple-element.14.near_ref, ...), custom_call_target="tpu_custom_call" | custom-call | tf_op jit(solution)/shard_map/update/pallas_call | solution.py:329
  59.2 0.0 all-to-all-done
  59.3 0.0 copy-start
  59.3 0.7 %copy-done = bf16[8,32,384]{2,1,0:T(8,128)(2,1)} copy-done((bf16[8,32,384]{2,1,0:T(8,128)(2,1)}, bf16[8,32,384]{2,1,0:T(8,128)(2,1)S(1)}, u32[]{:S(2)}) %copy-start) | copy-done | bytes 196632
  59.9 2.0 %planes.1 = f32[384,256]{1,0:T(8,128)} custom-call(bf16[256,384]{1,0:T(8,128)(2,1)} %bitcast.11, bf16[256,256]{1,0:T(8,128)(2,1)} %constant.22.clone.table_ref), custom_call_target="tpu_custom_call" | custom-call | tf_op jit(solution)/shard_map/planes/pallas_call | solution.py:347
Async XLA Ops:
  9.1 4.8 %collective-permute-start = (bf16[128,384]{1,0:T(8,128)(2,1)}, bf16[128,384]{1,0:T(8,128)(2,1)S(1)}, u32[]{:S(2)}, u32[]{:S(2)}) collective-permute-start(bf16[128,384]{1,0:T(8,128)(2,1)} %get-tuple-element.10.pack_a_ref.refs_0_), channel_id=1, source_target_pairs={{0,8},{8,0},{16,24},{24,16},{1,9},{9,1},{17,25},{25,17},{2,10},{10... | collective-permute-start | bytes 294920 | tf_op jit(solution)/shard_map/ppermute | solution.py:297
  11.1 3.7 %collective-permute-start.1 = (bf16[128,384]{1,0:T(8,128)(2,1)}, bf16[128,384]{1,0:T(8,128)(2,1)S(1)}, u32[]{:S(2)}, u32[]{:S(2)}) collective-permute-start(bf16[128,384]{1,0:T(8,128)(2,1)} %get-tuple-element.11.pack_b_ref.refs_3_), channel_id=1, source_target_pairs={{0,16},{8,24},{16,0},{24,8},{1,17},{9,25},{17,1},{25,9},{2,18},{10... | collective-permute-start | bytes 294920 | tf_op jit(solution)/shard_map/ppermute | solution.py:297
  13.9 1.0 %copy-start.1 = (bf16[128,384]{1,0:T(8,128)(2,1)}, bf16[128,384]{1,0:T(8,128)(2,1)S(1)}, u32[]{:S(2)}) copy-start(bf16[128,384]{1,0:T(8,128)(2,1)S(1)} %collective-permute-done.got_a_ref.refs_1_) | copy-start | bytes 294916
  14.8 0.6 %copy-start.2 = (bf16[128,384]{1,0:T(8,128)(2,1)}, bf16[128,384]{1,0:T(8,128)(2,1)S(1)}, u32[]{:S(2)}) copy-start(bf16[128,384]{1,0:T(8,128)(2,1)S(1)} %collective-permute-done.1.got_b_ref.refs_4_) | copy-start | bytes 294916
  17.2 3.7 %collective-permute-start.2 = (bf16[128,384]{1,0:T(8,128)(2,1)}, bf16[128,384]{1,0:T(8,128)(2,1)S(1)}, u32[]{:S(2)}, u32[]{:S(2)}) collective-permute-start(bf16[128,384]{1,0:T(8,128)(2,1)} %get-tuple-element.12), channel_id=1, source_target_pairs={{0,16},{8,24},{16,0},{24,8},{1,17},{9,25},{17,1},{25,9},{2,18},{10... | collective-permute-start | bytes 294920 | tf_op jit(solution)/shard_map/ppermute | solution.py:297
  18.7 3.7 %collective-permute-start.3 = (bf16[128,384]{1,0:T(8,128)(2,1)}, bf16[128,384]{1,0:T(8,128)(2,1)S(1)}, u32[]{:S(2)}, u32[]{:S(2)}) collective-permute-start(bf16[128,384]{1,0:T(8,128)(2,1)} %get-tuple-element.13), channel_id=1, source_target_pairs={{0,8},{8,0},{16,24},{24,16},{1,9},{9,1},{17,25},{25,17},{2,10},{10... | collective-permute-start | bytes 294920 | tf_op jit(solution)/shard_map/ppermute | solution.py:297
  20.9 1.5 %copy-start.3 = (bf16[128,384]{1,0:T(8,128)(2,1)}, bf16[128,384]{1,0:T(8,128)(2,1)S(1)}, u32[]{:S(2)}) copy-start(bf16[128,384]{1,0:T(8,128)(2,1)S(1)} %collective-permute-done.2.refs_2_) | copy-start | bytes 294916
  22.3 0.6 %copy-start.4 = (bf16[128,384]{1,0:T(8,128)(2,1)}, bf16[128,384]{1,0:T(8,128)(2,1)S(1)}, u32[]{:S(2)}) copy-start(bf16[128,384]{1,0:T(8,128)(2,1)S(1)} %collective-permute-done.3.refs_5_) | copy-start | bytes 294916
  25.8 33.5 %all-to-all-start = ((bf16[8,32,384]{2,1,0:T(8,128)(2,1)}), bf16[8,32,384]{2,1,0:T(8,128)(2,1)S(1)}, u32[]{:S(2)}, u32[]{:S(2)}) async-start(bf16[8,32,384]{2,1,0:T(8,128)(2,1)} %get-tuple-element.15), calls=%async_computation | async-start | bytes 393216 | tf_op jit(solution)/shard_map/all_to_all | solution.py:326
  59.3 0.7 %copy-start = (bf16[8,32,384]{2,1,0:T(8,128)(2,1)}, bf16[8,32,384]{2,1,0:T(8,128)(2,1)S(1)}, u32[]{:S(2)}) copy-start(bf16[8,32,384]{2,1,0:T(8,128)(2,1)S(1)} %all-to-all-done) | copy-start | bytes 589828
where the time goes:
time: 62.6 us; the launch traced here: 61.9 us
  Pallas kernels  40.3 us (64%)
  starting transfers between devices  13.3 us (21%)
  waiting for transfers between devices  5.06 us (8%)
  local copies, waits for them, and re-layouts  1.93 us (3%)
  other arithmetic  0.65 us (1%)
  between operations  0.65 us (1%)
    pallas_call x1, Pallas kernels, shards(): pl.pallas_call(functools.partial(update_kernel, gain_polynomial(6), (leng...  25.3 us
    pallas_call x1, Pallas kernels, shards(): pl.pallas_call(sections_kernel, grid=(length_x // block_x,), in_specs=[pl...  8.45 us
    all_to_all x1, starting transfers between devices, shards(): lax.all_to_all(pieces, 'slab', split_axis=0, concat_axis=0, tiled=True)  8.19 us
    ppermute x4, starting transfers between devices, hop(): lax.ppermute(value, 'rect', [(j, j ^ step) for j in range(rect_count)])  5.15 us
    ppermute x4, waiting for transfers between devices, hop(): lax.ppermute(value, 'rect', [(j, j ^ step) for j in range(rect_count)])  5.05 us
    pallas_call x1, Pallas kernels, shards(): pl.pallas_call(functools.partial(forces_kernel, routed), in_specs=[smem()...  2.78 us
    pallas_call x1, Pallas kernels, shards(): pl.pallas_call(planes_kernel, out_shape=jax.ShapeDtypeStruct((PLANES * lo...  2 us
    unnamed x10, local copies, waits for them, and re-layouts  1.93 us
  transfers between devices with their start and end apart: 5, of which 4 were waited for; matrix products, arithmetic and copies ran while one was open for 1% of the time, Pallas kernels for 41%

commit v1 on v0

--- a/solution.py
+++ b/solution.py
@@ -89,29 +89,63 @@
     return plane < 3
 
 
-def sections_kernel(now_ref, columns_ref, z_ref, *pack_refs):
-    rows = now_ref.shape[0]
+def gather_rows(section, row_of_lane, sublane):
+    values = jnp.where((row_of_lane < 8)[None], section[:, :8], section[:, 8:])
+    for distance in (4, 2, 1):
+        count = values.shape[0] // 2
+        first, second = values[:count], values[count:]
+        early = ((sublane & distance) == 0)[None]
+        late_row = ((row_of_lane & distance) != 0)[None]
+        if distance == 4:
+            kept = jnp.where(early, first, second)
+            moved = pltpu.roll(jnp.where(early, second, first), 4, 1)
+            values = jnp.where(early != late_row, kept, moved)
+        else:
+            up = pltpu.roll(first, 8 - distance, 1)
+            down = pltpu.roll(second, distance, 1)
+            values = jnp.where(early, jnp.where(late_row, up, first), jnp.where(late_row, second, down))
+    return values[0]
+
+
+def sections_kernel(now_ref, columns_ref, z_ref, *refs):
+    *pack_refs, now_vmem, arrivals = refs
     count = len(pack_refs)
-    group_x = rows // 4
-    mask = row_mask()[None]
-    lane = lax.broadcasted_iota(jnp.int32, (group_x, LANES), 1)
-    halves = [[] for _ in pack_refs]
-    for part in range(4):
-        block = now_ref[part * group_x : (part + 1) * group_x]
-        flat = block.reshape(group_x * block.shape[1], block.shape[2])
-        section = jnp.dot(flat, columns_ref[...], preferred_element_type=jnp.float32)
-        section = section.reshape(group_x, count, GROUP, LANES)
-        for half in range(count):
-            picked = jnp.sum(jnp.where(mask, section[:, half], 0.0), axis=1)
-            picked = picked.astype(jnp.bfloat16)
-            z_ref[part * group_x : (part + 1) * group_x, half * LANES : (half + 1) * LANES] = picked
-            halves[half].append(picked.astype(jnp.float32))
-    for half, pack_ref in enumerate(pack_refs):
-        for tile in range(3):
-            moved = pltpu.roll(halves[half][3], USED - 32 * tile, 1)
-            pack_ref[:, tile * LANES : (tile + 1) * LANES] = jnp.where(
-                lane < USED, halves[half][tile], moved
-            ).astype(jnp.bfloat16)
+    chunks = arrivals.shape[0]
+    length = now_ref.shape[0] // chunks
+
+    def fetch(chunk):
+        rows = pl.ds(chunk * length, length)
+        return pltpu.make_async_copy(now_ref.at[rows], now_vmem.at[rows], arrivals.at[chunk])
+
+    for chunk in range(chunks):
+        fetch(chunk).start()
+    sublane = lax.broadcasted_iota(jnp.int32, (8, LANES), 0)
+    row_of_lane = lax.broadcasted_iota(jnp.int32, (8, LANES), 1) % GROUP
+    lane = lax.broadcasted_iota(jnp.int32, (GROUP, LANES), 1)
+
+    def body(step, carry):
+        fetch(step).wait()
+        halves = [[] for _ in pack_refs]
+        for part in range(4):
+            rows = pl.ds((step * 4 + part) * GROUP, GROUP)
+            flat = now_vmem[rows].reshape(GROUP * now_vmem.shape[1], now_vmem.shape[2])
+            section = jnp.dot(flat, columns_ref[...], preferred_element_type=jnp.float32)
+            section = section.reshape(GROUP, count, GROUP, LANES)
+            for half in range(count):
+                picked = jnp.concatenate(
+                    [gather_rows(section[i : i + 8, half], row_of_lane, sublane) for i in range(0, GROUP, 8)], axis=0
+                ).astype(jnp.bfloat16)
+                z_ref[rows, half * LANES : (half + 1) * LANES] = picked
+                halves[half].append(picked.astype(jnp.float32))
+        for half, pack_ref in enumerate(pack_refs):
+            for tile in range(3):
+                moved = pltpu.roll(halves[half][3], USED - 32 * tile, 1)
+                pack_ref[pl.ds(step * GROUP, GROUP), tile * LANES : (tile + 1) * LANES] = jnp.where(
+                    lane < USED, halves[half][tile], moved
+                ).astype(jnp.bfloat16)
+        return carry
+
+    lax.fori_loop(0, chunks, body, 0)
 
 
 def neighbours(face_ref, rect):
@@ -122,8 +156,8 @@
     return partner, source
 
 
-def forward_kernel(face_ref, place_ref, pack_a_ref, pack_b_ref, got_a_ref, got_b_ref, send_a_ref, send_b_ref):
-    rect = place_ref[0]
+def forward_kernel(face_ref, pack_a_ref, pack_b_ref, got_a_ref, got_b_ref, send_a_ref, send_b_ref):
+    rect = lax.axis_index("rect")
     lower = packed_lower_mask(pack_a_ref.shape)
     for step, pack_ref, got_ref, send_ref in (
         (2, pack_a_ref, got_a_ref, send_a_ref),
@@ -141,11 +175,11 @@
     return jnp.where(code == 0, first, jnp.where(code == 1, second, third))
 
 
-def forces_kernel(routed, face_ref, place_ref, z_ref, *refs):
+def forces_kernel(routed, face_ref, z_ref, *refs):
     own_refs, one_refs, two_refs = [refs[i : len(refs) - 3 : 3] for i in range(3)]
     table_ref, near_ref, piece_ref = refs[-3:]
     count = len(own_refs)
-    rect = place_ref[0]
+    rect = lax.axis_index("rect")
     partner, source = neighbours(face_ref, rect)
     packed_rows = own_refs[0].shape[0]
     lower = packed_lower_mask(own_refs[0].shape)
@@ -205,41 +239,113 @@
             )
 
 
-def update_kernel(poly, sides, place_ref, now_ref, prev_ref, z_ref, near_ref, mix_ref, planes_ref, out_ref, force_ref):
-    rows, local_y, depth_z = now_ref.shape
-    step = pl.program_id(0)
-    slab = place_ref[1]
+def update_kernel(poly, sides, now_ref, prev_ref, z_ref, near_ref, mix_ref, planes_ref, out_ref, *scratch):
+    now_vmem, prev_vmem, out_vmem, force_a, force_b, modes_ref, square_ref, arrivals, departures = scratch
+    length_x, local_y, depth_z = now_vmem.shape
+    chunks = departures.shape[0]
+    length = length_x // chunks
+
+    def rows_of(chunk):
+        return pl.ds(chunk * length, length)
+
+    def fetch(chunk):
+        rows = rows_of(chunk)
+        return [
+            pltpu.make_async_copy(now_ref.at[rows], now_vmem.at[rows], arrivals.at[0, chunk]),
+            pltpu.make_async_copy(prev_ref.at[rows], prev_vmem.at[rows], arrivals.at[1, chunk]),
+        ]
+
+    def send(chunk):
+        rows = rows_of(chunk)
+        return pltpu.make_async_copy(out_vmem.at[rows], out_ref.at[rows], departures.at[chunk])
+
+    for chunk in range(chunks):
+        for copy in fetch(chunk):
+            copy.start()
     mask = row_mask()[None]
     for half in range(local_y // GROUP):
         cols = slice(half * LANES, (half + 1) * LANES)
         both = jnp.concatenate([z_ref[:, cols], near_ref[:, cols]], axis=1)
-        modes = jnp.dot(
+        modes_ref[:, cols] = jnp.dot(
             jnp.concatenate([both, both, both], axis=1), mix_ref[...], preferred_element_type=jnp.float32
         )
-        spread = jnp.where(mask, jnp.broadcast_to(modes[:, None, :], (rows, GROUP, LANES)), 0.0)
-        spread = spread.astype(jnp.bfloat16).reshape(rows * GROUP, LANES)
-        force = jnp.dot(spread, planes_ref[...], preferred_element_type=jnp.float32)
-        force_ref[:, half * GROUP : (half + 1) * GROUP, :] = force.reshape(rows, GROUP, depth_z)
     scale = math.pi * math.pi / 3.0
-    y_index = lax.broadcasted_iota(jnp.int32, (local_y, depth_z), 0) + slab * local_y
+    y_index = lax.broadcasted_iota(jnp.int32, (local_y, depth_z), 0) + lax.axis_index("slab") * local_y
     z_index = lax.broadcasted_iota(jnp.int32, (local_y, depth_z), 1)
-    y_part = y_index.astype(jnp.float32) / sides[1]
-    z_part = z_index.astype(jnp.float32) / sides[2]
-    base = scale * (y_part * y_part + z_part * z_part)
-
-    def body(row, carry):
-        x_index = jnp.full((1, 1), step * rows + row, jnp.int32)
-        x_part = x_index.astype(jnp.float32) / sides[0]
-        theta_sq = base + scale * (x_part * x_part)
-        gain = poly[-1] * theta_sq + poly[-2]
+    y_part = y_index.astype(jnp.float32) * (1.0 / sides[1])
+    z_part = z_index.astype(jnp.float32) * (1.0 / sides[2])
+    square_ref[...] = scale * (y_part * y_part + z_part * z_part)
+
+    def x_square(x):
+        part = x * (1.0 / sides[0])
+        return scale * (part * part)
+
+    def exact_gain(theta_sq):
+        value = poly[-1] * theta_sq + poly[-2]
         for coefficient in poly[-3::-1]:
-            gain = gain * theta_sq + coefficient
-        two_cos = 2.0 - theta_sq * gain
-        value = two_cos * now_ref[row].astype(jnp.float32) - prev_ref[row].astype(jnp.float32)
-        out_ref[row] = (value + gain * force_ref[row]).astype(jnp.bfloat16)
+            value = value * theta_sq + coefficient
+        return value
+
+    groups = length_x // GROUP
+
+    def make_force(group, force_ref):
+        row = jnp.minimum(group, groups - 1) * GROUP
+        for half in range(local_y // GROUP):
+            modes = modes_ref[pl.ds(row, GROUP), half * LANES : (half + 1) * LANES]
+            spread = jnp.where(mask, jnp.broadcast_to(modes[:, None, :], (GROUP, GROUP, LANES)), 0.0)
+            spread = spread.astype(jnp.bfloat16).reshape(GROUP * GROUP, LANES)
+            force = jnp.dot(spread, planes_ref[...], preferred_element_type=jnp.float32)
+            force_ref[:, half * GROUP : (half + 1) * GROUP, :] = force.reshape(GROUP, GROUP, depth_z)
+
+    middle = 0.5 * (GROUP - 1)
+    reach = middle - 1.0
+    begin, after = -middle / reach, (1.0 - middle) / reach
+
+    def advance(group, force_ref):
+        row = group * GROUP
+        first = row.astype(jnp.float32)
+        nodes = [x_square(first + (middle + offset)) for offset in (-reach, 0.0, reach)]
+        x_sq = [x_square(first + float(step)) for step in range(GROUP)]
+        for y_at in range(0, local_y, GROUP):
+            for z_at in range(0, depth_z, LANES):
+                tile = (slice(y_at, y_at + GROUP), slice(z_at, z_at + LANES))
+                yz_sq = square_ref[tile]
+                low, mid, high = [exact_gain(yz_sq + node) for node in nodes]
+                slope = (high - low) * 0.5
+                bend = (high + low) * 0.5 - mid
+                gain = mid + begin * slope + (begin * begin) * bend
+                rise = slope * (1.0 / reach) + bend * (after * after - begin * begin)
+                turn = bend * (2.0 / (reach * reach))
+                for step in range(GROUP):
+                    at = (row + step,) + tile
+                    two_cos = 2.0 - (yz_sq + x_sq[step]) * gain
+                    value = two_cos * now_vmem[at].astype(jnp.float32) - prev_vmem[at].astype(jnp.float32)
+                    out_vmem[at] = (value + gain * force_ref[(step,) + tile]).astype(jnp.bfloat16)
+                    gain = gain + rise
+                    rise = rise + turn
+
+    make_force(0, force_a)
+    pairs = length // (2 * GROUP)
+
+    def whole(chunk, carry):
+        for copy in fetch(chunk):
+            copy.wait()
+
+        def pair(index, inner):
+            group = (chunk * pairs + index) * 2
+            make_force(group + 1, force_b)
+            advance(group, force_a)
+            make_force(group + 2, force_a)
+            advance(group + 1, force_b)
+            return inner
+
+        lax.fori_loop(0, pairs, pair, 0)
+        send(chunk).start()
         return carry
 
-    lax.fori_loop(0, rows, body, 0, unroll=2)
+    lax.fori_loop(0, chunks, whole, 0)
+    for chunk in range(chunks):
+        send(chunk).wait()
 
 
 def planes_kernel(arrived_ref, table_ref, out_ref):
@@ -253,10 +359,21 @@
     return pl.BlockSpec(memory_space=pltpu.SMEM)
 
 
+def vmem():
+    return pl.BlockSpec(memory_space=pltpu.VMEM)
+
+
+def hbm():
+    return pl.BlockSpec(memory_space=pltpu.HBM)
+
+
+def limit(mib):
+    return pltpu.CompilerParams(vmem_limit_bytes=mib << 20)
+
+
 def shards(modes_now, modes_prev, face_partner):
     slab_count = lax.axis_size("slab")
     rect_count = lax.axis_size("rect")
-    slab_rank = lax.axis_index("slab")
     rect_rank = lax.axis_index("rect")
     _, length_x, local_y, depth_z = modes_now.shape
     length_y = local_y * slab_count
@@ -264,29 +381,26 @@
     assert local_y % GROUP == 0 and length_x % (4 * GROUP) == 0
     count = local_y // GROUP
     bf = jnp.bfloat16
-    place = jnp.stack([rect_rank, slab_rank]).astype(jnp.int32)
-    current = modes_now[0]
-    earlier = modes_prev[0]
+    current = pltpu.with_memory_space_constraint(modes_now[0], pltpu.HBM)
+    earlier = pltpu.with_memory_space_constraint(modes_prev[0], pltpu.HBM)
     columns = jnp.asarray(spread_columns(depth_z))
     planes = jnp.asarray(np.ascontiguousarray(spread_columns(depth_z).T))
     mix = jnp.asarray(force_matrix())
     table_x = jnp.asarray(cosine_table(length_x).astype(bf16))
     table_y = jnp.asarray(cosine_table(length_y).astype(bf16))
 
-    block_x = 4 * GROUP
     packed = jax.ShapeDtypeStruct((length_x // 4, 3 * LANES), bf)
+    chunks = 16
     z_own, *packs = pl.pallas_call(
         sections_kernel,
-        grid=(length_x // block_x,),
-        in_specs=[
-            pl.BlockSpec((block_x, local_y, depth_z), lambda i: (i, 0, 0)),
-            pl.BlockSpec((depth_z, LANES), lambda i: (0, 0)),
+        in_specs=[hbm(), vmem()],
+        out_specs=[vmem()] * (1 + count),
+        out_shape=[jax.ShapeDtypeStruct((length_x, count * LANES), bf)] + [packed] * count,
+        scratch_shapes=[
+            pltpu.VMEM((length_x, local_y, depth_z), bf),
+            pltpu.SemaphoreType.DMA((length_x // (4 * GROUP),)),
         ],
-        out_specs=[
-            pl.BlockSpec((block_x, count * LANES), lambda i: (i, 0)),
-            *[pl.BlockSpec((GROUP, 3 * LANES), lambda i: (i, 0)) for _ in range(count)],
-        ],
-        out_shape=[jax.ShapeDtypeStruct((length_x, count * LANES), bf)] + [packed] * count,
+        compiler_params=limit(16),
         name="sections",
     )(current, columns)
 
@@ -299,10 +413,12 @@
         ones = [hop(packs[0], 1), hop(packs[1], 2)]
         sends = pl.pallas_call(
             forward_kernel,
-            in_specs=[smem(), smem()] + [pl.BlockSpec() for _ in range(4)],
+            in_specs=[smem()] + [vmem()] * 4,
+            out_specs=[vmem()] * 2,
             out_shape=[packed, packed],
+            compiler_params=limit(8),
             name="forward",
-        )(face_partner, place, *packs, *ones)
+        )(face_partner, *packs, *ones)
         twos = [hop(sends[0], 2), hop(sends[1], 1)]
     else:
         rect_ids = jnp.arange(rect_count, dtype=jnp.int32)
@@ -315,38 +431,42 @@
 
     near, pieces = pl.pallas_call(
         functools.partial(forces_kernel, routed),
-        in_specs=[smem(), smem()] + [pl.BlockSpec() for _ in range(2 + len(routes))],
+        in_specs=[smem()] + [vmem()] * (2 + len(routes)),
+        out_specs=[vmem()] * 2,
         out_shape=[
             jax.ShapeDtypeStruct((length_x, count * LANES), bf),
             jax.ShapeDtypeStruct((slab_count, local_y, PLANES * local_x), bf),
         ],
+        compiler_params=limit(8),
         name="forces",
-    )(face_partner, place, z_own, *routes, table_x)
+    )(face_partner, z_own, *routes, table_x)
 
     arrived = lax.all_to_all(pieces, "slab", split_axis=0, concat_axis=0, tiled=True)
 
-    rows = 32
+    wide = (length_x, local_y, depth_z)
     fresh = pl.pallas_call(
-        functools.partial(update_kernel, gain_polynomial(6), (length_x, length_y, depth_z)),
-        grid=(length_x // rows,),
-        in_specs=[
-            smem(),
-            pl.BlockSpec((rows, local_y, depth_z), lambda i: (i, 0, 0)),
-            pl.BlockSpec((rows, local_y, depth_z), lambda i: (i, 0, 0)),
-            pl.BlockSpec((rows, count * LANES), lambda i: (i, 0)),
-            pl.BlockSpec((rows, count * LANES), lambda i: (i, 0)),
-            pl.BlockSpec(mix.shape, lambda i: (0, 0)),
-            pl.BlockSpec(planes.shape, lambda i: (0, 0)),
+        functools.partial(update_kernel, gain_polynomial(5), (length_x, length_y, depth_z)),
+        in_specs=[hbm(), hbm()] + [vmem()] * 4,
+        out_specs=hbm(),
+        out_shape=jax.ShapeDtypeStruct(wide, bf),
+        scratch_shapes=[
+            *[pltpu.VMEM(wide, bf)] * 3,
+            *[pltpu.VMEM((GROUP, local_y, depth_z), jnp.float32)] * 2,
+            pltpu.VMEM((length_x, count * LANES), jnp.float32),
+            pltpu.VMEM((local_y, depth_z), jnp.float32),
+            pltpu.SemaphoreType.DMA((2, chunks)),
+            pltpu.SemaphoreType.DMA((chunks,)),
         ],
-        out_specs=pl.BlockSpec((rows, local_y, depth_z), lambda i: (i, 0, 0)),
-        out_shape=jax.ShapeDtypeStruct((length_x, local_y, depth_z), bf),
-        scratch_shapes=[pltpu.VMEM((rows, local_y, depth_z), jnp.float32)],
+        compiler_params=limit(40),
         name="update",
-    )(place, current, earlier, z_own, near, mix, planes)
+    )(current, earlier, z_own, near, mix, planes)
 
     forcing = pl.pallas_call(
         planes_kernel,
+        in_specs=[vmem()] * 2,
+        out_specs=vmem(),
         out_shape=jax.ShapeDtypeStruct((PLANES * local_x, length_y), jnp.float32),
+        compiler_params=limit(8),
         name="planes",
     )(arrived.reshape(length_y, PLANES * local_x), table_y)
     return (fresh[None], forcing.reshape(1, PLANES, local_x, length_y))

time: 62.6 us -> 42.7 us (0.68)
  Pallas kernels: 40.3 us -> 22 us
  local copies, waits for them, and re-layouts: 1.93 us -> 0.93 us
  other arithmetic: 0.65 us -> 0 us
    pallas_call x4, Pallas kernels: 37.5 us -> 20.1 us  [the longest x1 13 us: shards(): pl.pallas_call(functools.partial(update_kernel, gain_polynomial(5), (leng...]
    unnamed x10 -> x12, local copies, waits for them, and re-layouts: 1.93 us -> 0.93 us
    pallas_call x1, Pallas kernels: 2.78 us -> 1.96 us  [shards(): pl.pallas_call(functools.partial(forces_kernel, routed), in_specs=[smem()...]
    another operation x1 -> x0, other arithmetic: 0.65 us -> none  [shards(): place = jnp.stack([rect_rank, slab_rank]).astype(jnp.int32)]
  transfers between devices with their start and end apart: 5 -> 5, of which waited for: 4 -> 4; matrix products, arithmetic and copies ran while one was open for 1% -> 0% of each run, Pallas kernels for 41% -> 31%
where the time goes in v1:
time: 42.7 us; the launch traced here: 42.4 us
  Pallas kernels  22 us (52%)
  starting transfers between devices  13.4 us (31%)
  waiting for transfers between devices  5.37 us (13%)
  local copies, waits for them, and re-layouts  0.93 us (2%)
  between operations  0.72 us (2%)
    pallas_call x1, Pallas kernels, shards(): pl.pallas_call(functools.partial(update_kernel, gain_polynomial(5), (leng...  13 us
    all_to_all x1, starting transfers between devices, shards(): lax.all_to_all(pieces, 'slab', split_axis=0, concat_axis=0, tiled=True)  8.19 us
    pallas_call x1, Pallas kernels, shards(): pl.pallas_call(sections_kernel, in_specs=[hbm(), vmem()], out_specs=[vmem...  5.46 us
    ppermute x4, waiting for transfers between devices, hop(): lax.ppermute(value, 'rect', [(j, j ^ step) for j in range(rect_count)])  5.36 us
    ppermute x4, starting transfers between devices, hop(): lax.ppermute(value, 'rect', [(j, j ^ step) for j in range(rect_count)])  5.2 us
    pallas_call x1, Pallas kernels, shards(): pl.pallas_call(functools.partial(forces_kernel, routed), in_specs=[smem()...  1.96 us
    pallas_call x1, Pallas kernels, shards(): pl.pallas_call(planes_kernel, in_specs=[vmem()] * 2, out_specs=vmem(), ou...  1 us
    unnamed x12, local copies, waits for them, and re-layouts  0.93 us
  transfers between devices with their start and end apart: 5, of which 4 were waited for; matrix products, arithmetic and copies ran while one was open for 0% of the time, Pallas kernels for 31%

profile of v1, /device:TPU:1, one launch (start us, length us, event | category | flops | bytes accessed | tf_op | source)
XLA Modules:
  0.0 42.4 jit_solution(12841175365276309719)
XLA Ops:
  0.6 0.0 copy-start
  0.6 0.0 copy-start.3
  0.7 0.0 copy-start.1
  0.7 0.0 copy-start.4
  0.7 0.9 %copy-done.4 = bf16[256,128]{1,0:T(8,128)(2,1)S(1)} copy-done((bf16[256,128]{1,0:T(8,128)(2,1)S(1)}, bf16[256,128]{1,0:T(8,128)(2,1)}, u32[]{:S(2)}) %copy-start.4) | copy-done | bytes 65560
  1.6 0.0 copy-start.5
  1.6 5.5 %sections.1 = (bf16[512,256]{1,0:T(8,128)(2,1)S(1)}, bf16[128,384]{1,0:T(8,128)(2,1)S(1)}, bf16[128,384]{1,0:T(8,128)(2,1)S(1)}) custom-call(bf16[512,32,256]{2,1,0:T(8,128)(2,1)} %bitcast.6, bf16[256,128]{1,0:T(8,128)(2,1)S(1)} %copy-done.4), custom_call_target="tpu_custom_call" | custom-call | tf_op jit(solution)/shard_map/sections/pallas_call | solution.py:394
  7.0 2.1 %collective-permute-start = (bf16[128,384]{1,0:T(8,128)(2,1)S(1)}, bf16[128,384]{1,0:T(8,128)(2,1)S(1)}, u32[]{:S(2)}, u32[]{:S(2)}) collective-permute-start(bf16[128,384]{1,0:T(8,128)(2,1)S(1)} %get-tuple-element.10.pack_a_ref.refs_0_), channel_id=1, source_target_pairs={{0,8},{8,0},{16,24},{24,16},{1,9},{9,1},{17,25},{25,17},{2,10},{10... | collective-permute-start | bytes 294920 | tf_op jit(solution)/shard_map/ppermute | solution.py:411
  9.2 1.2 %collective-permute-start.1 = (bf16[128,384]{1,0:T(8,128)(2,1)S(1)}, bf16[128,384]{1,0:T(8,128)(2,1)S(1)}, u32[]{:S(2)}, u32[]{:S(2)}) collective-permute-start(bf16[128,384]{1,0:T(8,128)(2,1)S(1)} %get-tuple-element.11.pack_b_ref.refs_3_), channel_id=1, source_target_pairs={{0,16},{8,24},{16,0},{24,8},{1,17},{9,25},{17,1},{25,9},{2,18},{10... | collective-permute-start | bytes 294920 | tf_op jit(solution)/shard_map/ppermute | solution.py:411
  10.4 1.3 %collective-permute-done.got_a_ref.refs_1_ = bf16[128,384]{1,0:T(8,128)(2,1)S(1)} collective-permute-done((bf16[128,384]{1,0:T(8,128)(2,1)S(1)}, bf16[128,384]{1,0:T(8,128)(2,1)S(1)}, u32[]{:S(2)}, u32[]{:S(2)}) %collective-permute-start) | collective-permute-done | bytes 98336 | tf_op jit(solution)/shard_map/ppermute | solution.py:411
  11.7 0.9 %collective-permute-done.1.got_b_ref.refs_4_ = bf16[128,384]{1,0:T(8,128)(2,1)S(1)} collective-permute-done((bf16[128,384]{1,0:T(8,128)(2,1)S(1)}, bf16[128,384]{1,0:T(8,128)(2,1)S(1)}, u32[]{:S(2)}, u32[]{:S(2)}) %collective-permute-start.1) | collective-permute-done | bytes 98336 | tf_op jit(solution)/shard_map/ppermute | solution.py:411
  12.6 0.0 copy-done.5
  12.6 0.6 %forward.1 = (bf16[128,384]{1,0:T(8,128)(2,1)S(1)}, bf16[128,384]{1,0:T(8,128)(2,1)S(1)}) custom-call(s32[4]{0:T(128)S(1)} %copy-done.5, bf16[128,384]{1,0:T(8,128)(2,1)S(1)} %get-tuple-element.10.pack_a_ref.refs_0_, bf16[128,384]{1,0:T(8,128)(2,1)S(1)} %get-tuple-element.11.pack_b_ref.refs_3_, bf16[128,384]{1,0:T(8,128)(2,1)S(1)} %collective-permute-done.got_a_ref.refs_1_, ...), custom_call_target="tpu_custom_call" | custom-call | tf_op jit(solution)/shard_map/forward/pallas_call | solution.py:414
  13.3 1.5 %collective-permute-start.2 = (bf16[128,384]{1,0:T(8,128)(2,1)S(1)}, bf16[128,384]{1,0:T(8,128)(2,1)S(1)}, u32[]{:S(2)}, u32[]{:S(2)}) collective-permute-start(bf16[128,384]{1,0:T(8,128)(2,1)S(1)} %get-tuple-element.12), channel_id=1, source_target_pairs={{0,16},{8,24},{16,0},{24,8},{1,17},{9,25},{17,1},{25,9},{2,18},{10... | collective-permute-start | bytes 294920 | tf_op jit(solution)/shard_map/ppermute | solution.py:411
  14.8 0.3 collective-permute-start.3
  15.1 1.7 %collective-permute-done.2.refs_2_ = bf16[128,384]{1,0:T(8,128)(2,1)S(1)} collective-permute-done((bf16[128,384]{1,0:T(8,128)(2,1)S(1)}, bf16[128,384]{1,0:T(8,128)(2,1)S(1)}, u32[]{:S(2)}, u32[]{:S(2)}) %collective-permute-start.2) | collective-permute-done | bytes 98336 | tf_op jit(solution)/shard_map/ppermute | solution.py:411
  16.8 1.5 %collective-permute-done.3.refs_5_ = bf16[128,384]{1,0:T(8,128)(2,1)S(1)} collective-permute-done((bf16[128,384]{1,0:T(8,128)(2,1)S(1)}, bf16[128,384]{1,0:T(8,128)(2,1)S(1)}, u32[]{:S(2)}, u32[]{:S(2)}) %collective-permute-start.3) | collective-permute-done | bytes 98336 | tf_op jit(solution)/shard_map/ppermute | solution.py:411
  18.2 0.0 copy-done
  18.3 2.0 %forces.1 = (bf16[512,256]{1,0:T(8,128)(2,1)S(1)}, bf16[8,32,384]{2,1,0:T(8,128)(2,1)}) custom-call(s32[4]{0:T(128)S(1)} %copy-done.5, bf16[512,256]{1,0:T(8,128)(2,1)S(1)} %get-tuple-element.9.z_ref, bf16[128,384]{1,0:T(8,128)(2,1)S(1)} %get-tuple-element.10.pack_a_ref.refs_0_, bf16[128,384]{1,0:T(8,128)(2,1)S(1)} %collective-permute-done.got_a_ref.refs_1_, ...), custom_call_target="tpu_custom_call" | custom-call | tf_op jit(solution)/shard_map/forces/pallas_call | solution.py:432
  20.2 8.2 %all-to-all-start = ((bf16[8,32,384]{2,1,0:T(8,128)(2,1)}), bf16[8,32,384]{2,1,0:T(8,128)(2,1)S(1)}, u32[]{:S(2)}, u32[]{:S(2)}) async-start(bf16[8,32,384]{2,1,0:T(8,128)(2,1)} %get-tuple-element.15), calls=%async_computation | async-start | bytes 393216 | tf_op jit(solution)/shard_map/all_to_all | solution.py:444
  28.4 0.0 copy-done.3
  28.4 0.0 copy-done.1
  28.4 0.0 copy-start.2
  28.4 13.0 %update.1 = bf16[512,32,256]{2,1,0:T(8,128)(2,1)} custom-call(bf16[512,32,256]{2,1,0:T(8,128)(2,1)} %bitcast.7, bf16[512,32,256]{2,1,0:T(8,128)(2,1)} %bitcast.8, bf16[512,256]{1,0:T(8,128)(2,1)S(1)} %get-tuple-element.9.z_ref, bf16[512,256]{1,0:T(8,128)(2,1)S(1)} %get-tuple-element.14.near_ref, bf16[768,128]{1,0:T(8,128)(2,1)S(1)} %copy-done.1, ...), custom_call_target="tpu_custom_call" | custom-call | tf_op jit(solution)/shard_map/update/pallas_call | solution.py:447
  41.4 0.0 all-to-all-done
  41.4 0.0 copy-done.2
  41.4 1.0 %planes.1 = f32[384,256]{1,0:T(8,128)} custom-call(bf16[256,384]{1,0:T(8,128)(2,1)S(1)} %bitcast.5, bf16[256,256]{1,0:T(8,128)(2,1)S(1)} %copy-done.2), custom_call_target="tpu_custom_call" | custom-call | tf_op jit(solution)/shard_map/planes/pallas_call | solution.py:464
Async XLA Ops:
  0.6 17.6 %copy-start = (bf16[512,512]{1,0:T(8,128)(2,1)S(1)}, bf16[512,512]{1,0:T(8,128)(2,1)}, u32[]{:S(2)}) copy-start(bf16[512,512]{1,0:T(8,128)(2,1)} %constant.13.clone.refs_6_) | copy-start | bytes 1572868
  0.6 27.8 %copy-start.3 = (bf16[128,256]{1,0:T(8,128)(2,1)S(1)}, bf16[128,256]{1,0:T(8,128)(2,1)}, u32[]{:S(2)}) copy-start(bf16[128,256]{1,0:T(8,128)(2,1)} %constant.11.clone.planes_ref) | copy-start | bytes 196612
  0.7 27.8 %copy-start.1 = (bf16[768,128]{1,0:T(8,128)(2,1)S(1)}, bf16[768,128]{1,0:T(8,128)(2,1)}, u32[]{:S(2)}) copy-start(bf16[768,128]{1,0:T(8,128)(2,1)} %constant.12.clone.mix_ref) | copy-start | bytes 589828
  0.7 0.9 %copy-start.4 = (bf16[256,128]{1,0:T(8,128)(2,1)S(1)}, bf16[256,128]{1,0:T(8,128)(2,1)}, u32[]{:S(2)}) copy-start(bf16[256,128]{1,0:T(8,128)(2,1)} %constant.10.clone.columns_ref) | copy-start | bytes 196612
  1.6 11.0 %copy-start.5 = (s32[4]{0:T(128)S(1)}, s32[4]{0:T(128)}, u32[]{:S(2)}) copy-start(s32[4]{0:T(128)} %face_ref.3) | copy-start | bytes 52
  7.0 4.6 %collective-permute-start = (bf16[128,384]{1,0:T(8,128)(2,1)S(1)}, bf16[128,384]{1,0:T(8,128)(2,1)S(1)}, u32[]{:S(2)}, u32[]{:S(2)}) collective-permute-start(bf16[128,384]{1,0:T(8,128)(2,1)S(1)} %get-tuple-element.10.pack_a_ref.refs_0_), channel_id=1, source_target_pairs={{0,8},{8,0},{16,24},{24,16},{1,9},{9,1},{17,25},{25,17},{2,10},{10... | collective-permute-start | bytes 294920 | tf_op jit(solution)/shard_map/ppermute | solution.py:411
  9.2 3.5 %collective-permute-start.1 = (bf16[128,384]{1,0:T(8,128)(2,1)S(1)}, bf16[128,384]{1,0:T(8,128)(2,1)S(1)}, u32[]{:S(2)}, u32[]{:S(2)}) collective-permute-start(bf16[128,384]{1,0:T(8,128)(2,1)S(1)} %get-tuple-element.11.pack_b_ref.refs_3_), channel_id=1, source_target_pairs={{0,16},{8,24},{16,0},{24,8},{1,17},{9,25},{17,1},{25,9},{2,18},{10... | collective-permute-start | bytes 294920 | tf_op jit(solution)/shard_map/ppermute | solution.py:411
  13.3 3.5 %collective-permute-start.2 = (bf16[128,384]{1,0:T(8,128)(2,1)S(1)}, bf16[128,384]{1,0:T(8,128)(2,1)S(1)}, u32[]{:S(2)}, u32[]{:S(2)}) collective-permute-start(bf16[128,384]{1,0:T(8,128)(2,1)S(1)} %get-tuple-element.12), channel_id=1, source_target_pairs={{0,16},{8,24},{16,0},{24,8},{1,17},{9,25},{17,1},{25,9},{2,18},{10... | collective-permute-start | bytes 294920 | tf_op jit(solution)/shard_map/ppermute | solution.py:411
  14.8 3.5 %collective-permute-start.3 = (bf16[128,384]{1,0:T(8,128)(2,1)S(1)}, bf16[128,384]{1,0:T(8,128)(2,1)S(1)}, u32[]{:S(2)}, u32[]{:S(2)}) collective-permute-start(bf16[128,384]{1,0:T(8,128)(2,1)S(1)} %get-tuple-element.13), channel_id=1, source_target_pairs={{0,8},{8,0},{16,24},{24,16},{1,9},{9,1},{17,25},{25,17},{2,10},{10... | collective-permute-start | bytes 294920 | tf_op jit(solution)/shard_map/ppermute | solution.py:411
  20.2 21.2 %all-to-all-start = ((bf16[8,32,384]{2,1,0:T(8,128)(2,1)}), bf16[8,32,384]{2,1,0:T(8,128)(2,1)S(1)}, u32[]{:S(2)}, u32[]{:S(2)}) async-start(bf16[8,32,384]{2,1,0:T(8,128)(2,1)} %get-tuple-element.15), calls=%async_computation | async-start | bytes 393216 | tf_op jit(solution)/shard_map/all_to_all | solution.py:444
  28.4 13.0 %copy-start.2 = (bf16[256,256]{1,0:T(8,128)(2,1)S(1)}, bf16[256,256]{1,0:T(8,128)(2,1)}, u32[]{:S(2)}) copy-start(bf16[256,256]{1,0:T(8,128)(2,1)} %constant.14.clone.table_ref) | copy-start | bytes 393220

commit v2 on v1

--- a/solution.py
+++ b/solution.py
@@ -38,6 +38,17 @@
     out = np.zeros((depth_z, LANES), bf16)
     out[:, :USED] = np.repeat(columns, GROUP, axis=1)
     return out
+
+
+def section_columns(depth_z):
+    mode = lax.broadcasted_iota(jnp.int32, (depth_z, LANES), 0)
+    lane = lax.broadcasted_iota(jnp.int32, (depth_z, LANES), 1)
+    plane = lane // GROUP
+    cell = jnp.where(plane < 3, plane, depth_z - PLANES + plane)
+    phase = mode * (2 * cell + 1) % (4 * depth_z)
+    angle = phase.astype(jnp.float32) * (math.pi / (2.0 * depth_z))
+    weight = jnp.where(mode == 0, math.sqrt(1.0 / depth_z), math.sqrt(2.0 / depth_z))
+    return jnp.where(lane < USED, weight * jnp.cos(angle), 0.0).astype(jnp.bfloat16)
 
 
 def force_matrix():
@@ -107,9 +118,9 @@
     return values[0]
 
 
-def sections_kernel(now_ref, columns_ref, z_ref, *refs):
-    *pack_refs, now_vmem, arrivals = refs
-    count = len(pack_refs)
+def sections_kernel(now_ref, z_ref, pack_ref, now_vmem, arrivals):
+    count = now_ref.shape[1] // GROUP
+    packed_rows = now_ref.shape[0] // 4
     chunks = arrivals.shape[0]
     length = now_ref.shape[0] // chunks
 
@@ -119,17 +130,18 @@
 
     for chunk in range(chunks):
         fetch(chunk).start()
+    columns = section_columns(now_ref.shape[2])
     sublane = lax.broadcasted_iota(jnp.int32, (8, LANES), 0)
     row_of_lane = lax.broadcasted_iota(jnp.int32, (8, LANES), 1) % GROUP
     lane = lax.broadcasted_iota(jnp.int32, (GROUP, LANES), 1)
 
     def body(step, carry):
         fetch(step).wait()
-        halves = [[] for _ in pack_refs]
+        halves = [[] for _ in range(count)]
         for part in range(4):
             rows = pl.ds((step * 4 + part) * GROUP, GROUP)
             flat = now_vmem[rows].reshape(GROUP * now_vmem.shape[1], now_vmem.shape[2])
-            section = jnp.dot(flat, columns_ref[...], preferred_element_type=jnp.float32)
+            section = jnp.dot(flat, columns, preferred_element_type=jnp.float32)
             section = section.reshape(GROUP, count, GROUP, LANES)
             for half in range(count):
                 picked = jnp.concatenate(
@@ -137,10 +149,10 @@
                 ).astype(jnp.bfloat16)
                 z_ref[rows, half * LANES : (half + 1) * LANES] = picked
                 halves[half].append(picked.astype(jnp.float32))
-        for half, pack_ref in enumerate(pack_refs):
+        for half in range(count):
             for tile in range(3):
                 moved = pltpu.roll(halves[half][3], USED - 32 * tile, 1)
-                pack_ref[pl.ds(step * GROUP, GROUP), tile * LANES : (tile + 1) * LANES] = jnp.where(
+                pack_ref[pl.ds(half * packed_rows + step * GROUP, GROUP), tile * LANES : (tile + 1) * LANES] = jnp.where(
                     lane < USED, halves[half][tile], moved
                 ).astype(jnp.bfloat16)
         return carry
@@ -156,44 +168,18 @@
     return partner, source
 
 
-def forward_kernel(face_ref, pack_a_ref, pack_b_ref, got_a_ref, got_b_ref, send_a_ref, send_b_ref):
-    rect = lax.axis_index("rect")
-    lower = packed_lower_mask(pack_a_ref.shape)
-    for step, pack_ref, got_ref, send_ref in (
-        (2, pack_a_ref, got_a_ref, send_a_ref),
-        (1, pack_b_ref, got_b_ref, send_b_ref),
-    ):
-        partner, source = neighbours(face_ref, rect ^ step)
-        own = pack_ref[...].astype(jnp.float32)
-        got = got_ref[...].astype(jnp.float32)
-        for_lower = jnp.where(partner == rect, own, got)
-        for_upper = jnp.where(source == rect, own, got)
-        send_ref[...] = jnp.where(lower, for_lower, for_upper).astype(jnp.bfloat16)
-
-
-def pick(code, first, second, third):
-    return jnp.where(code == 0, first, jnp.where(code == 1, second, third))
-
-
-def forces_kernel(routed, face_ref, z_ref, *refs):
-    own_refs, one_refs, two_refs = [refs[i : len(refs) - 3 : 3] for i in range(3)]
-    table_ref, near_ref, piece_ref = refs[-3:]
-    count = len(own_refs)
-    rect = lax.axis_index("rect")
-    partner, source = neighbours(face_ref, rect)
-    packed_rows = own_refs[0].shape[0]
-    lower = packed_lower_mask(own_refs[0].shape)
+def forces_kernel(face_ref, z_ref, every_ref, table_ref, near_ref, piece_ref):
+    count = z_ref.shape[1] // LANES
+    partner, source = neighbours(face_ref, lax.axis_index("rect"))
+    packed_rows = every_ref.shape[1] // count
+    lower = packed_lower_mask((packed_rows, every_ref.shape[2]))
     blocks = packed_rows // GROUP
     lane = lax.broadcasted_iota(jnp.int32, (blocks, GROUP, LANES), 2)
-    for half, (own_ref, one_ref, two_ref) in enumerate(zip(own_refs, one_refs, two_refs)):
-        if routed:
-            step = half + 1
-            code_lower = jnp.where(partner == rect, 0, jnp.where(partner == (rect ^ step), 1, 2))
-            code_upper = jnp.where(source == rect, 0, jnp.where(source == (rect ^ step), 1, 2))
-        else:
-            code_lower, code_upper = jnp.int32(1), jnp.int32(2)
-        values = [ref[...].astype(jnp.float32) for ref in (own_ref, one_ref, two_ref)]
-        packed = jnp.where(lower, pick(code_lower, *values), pick(code_upper, *values))
+    for half in range(count):
+        rows = pl.ds(half * packed_rows, packed_rows)
+        packed = jnp.where(
+            lower, every_ref[partner, rows].astype(jnp.float32), every_ref[source, rows].astype(jnp.float32)
+        )
         tiles = [
             packed[:, tile * LANES : (tile + 1) * LANES].reshape(blocks, GROUP, LANES) for tile in range(3)
         ]
@@ -373,8 +359,6 @@
 
 def shards(modes_now, modes_prev, face_partner):
     slab_count = lax.axis_size("slab")
-    rect_count = lax.axis_size("rect")
-    rect_rank = lax.axis_index("rect")
     _, length_x, local_y, depth_z = modes_now.shape
     length_y = local_y * slab_count
     local_x = length_x // slab_count
@@ -383,55 +367,32 @@
     bf = jnp.bfloat16
     current = pltpu.with_memory_space_constraint(modes_now[0], pltpu.HBM)
     earlier = pltpu.with_memory_space_constraint(modes_prev[0], pltpu.HBM)
-    columns = jnp.asarray(spread_columns(depth_z))
     planes = jnp.asarray(np.ascontiguousarray(spread_columns(depth_z).T))
     mix = jnp.asarray(force_matrix())
     table_x = jnp.asarray(cosine_table(length_x).astype(bf16))
     table_y = jnp.asarray(cosine_table(length_y).astype(bf16))
 
-    packed = jax.ShapeDtypeStruct((length_x // 4, 3 * LANES), bf)
     chunks = 16
-    z_own, *packs = pl.pallas_call(
+    z_own, pack = pl.pallas_call(
         sections_kernel,
-        in_specs=[hbm(), vmem()],
-        out_specs=[vmem()] * (1 + count),
-        out_shape=[jax.ShapeDtypeStruct((length_x, count * LANES), bf)] + [packed] * count,
+        in_specs=[hbm()],
+        out_specs=[vmem()] * 2,
+        out_shape=[
+            jax.ShapeDtypeStruct((length_x, count * LANES), bf),
+            jax.ShapeDtypeStruct((count * length_x // 4, 3 * LANES), bf),
+        ],
         scratch_shapes=[
             pltpu.VMEM((length_x, local_y, depth_z), bf),
             pltpu.SemaphoreType.DMA((length_x // (4 * GROUP),)),
         ],
         compiler_params=limit(16),
         name="sections",
-    )(current, columns)
-
-    routed = rect_count == 4 and count == 2
-    if routed:
-
-        def hop(value, step):
-            return lax.ppermute(value, "rect", [(j, j ^ step) for j in range(rect_count)])
-
-        ones = [hop(packs[0], 1), hop(packs[1], 2)]
-        sends = pl.pallas_call(
-            forward_kernel,
-            in_specs=[smem()] + [vmem()] * 4,
-            out_specs=[vmem()] * 2,
-            out_shape=[packed, packed],
-            compiler_params=limit(8),
-            name="forward",
-        )(face_partner, *packs, *ones)
-        twos = [hop(sends[0], 2), hop(sends[1], 1)]
-    else:
-        rect_ids = jnp.arange(rect_count, dtype=jnp.int32)
-        partner = jnp.sum(jnp.where(rect_ids == rect_rank, face_partner, 0))
-        source = jnp.sum(jnp.where(face_partner == rect_rank, rect_ids, 0))
-        every = [lax.all_gather(pack, "rect", axis=0) for pack in packs]
-        ones = [lax.dynamic_index_in_dim(value, partner, 0, keepdims=False) for value in every]
-        twos = [lax.dynamic_index_in_dim(value, source, 0, keepdims=False) for value in every]
-    routes = [value for triple in zip(packs, ones, twos) for value in triple]
-
+    )(current)
+
+    every = lax.all_gather(pack, "rect", axis=0)
     near, pieces = pl.pallas_call(
-        functools.partial(forces_kernel, routed),
-        in_specs=[smem()] + [vmem()] * (2 + len(routes)),
+        forces_kernel,
+        in_specs=[smem()] + [vmem()] * 3,
         out_specs=[vmem()] * 2,
         out_shape=[
             jax.ShapeDtypeStruct((length_x, count * LANES), bf),
@@ -439,7 +400,7 @@
         ],
         compiler_params=limit(8),
         name="forces",
-    )(face_partner, z_own, *routes, table_x)
+    )(face_partner, z_own, every, table_x)
 
     arrived = lax.all_to_all(pieces, "slab", split_axis=0, concat_axis=0, tiled=True)
 

time: 42.7 us -> 40 us (0.937)
  blocking collectives: 0 us -> 10.2 us
  starting transfers between devices: 13.4 us -> 7.34 us
  waiting for transfers between devices: 5.37 us -> 0.01 us
  local copies, waits for them, and re-layouts: 0.93 us -> 0.03 us
  Pallas kernels: 22 us -> 21.4 us
    all_gather x0 -> x1, blocking collectives: none -> 10.2 us  [shards(): every = lax.all_gather(pack, 'rect', axis=0)]
    ppermute x4 -> x0, waiting for transfers between devices: 5.36 us -> none  [hop(): lax.ppermute(value, 'rect', [(j, j ^ step) for j in range(rect_count)])]
    ppermute x4 -> x0, starting transfers between devices: 5.2 us -> none  [hop(): lax.ppermute(value, 'rect', [(j, j ^ step) for j in range(rect_count)])]
    unnamed x12 -> x10, local copies, waits for them, and re-layouts: 0.93 us -> 0.03 us
    all_to_all x1, starting transfers between devices: 8.19 us -> 7.34 us  [shards(): lax.all_to_all(pieces, 'slab', split_axis=0, concat_axis=0, tiled=True)]
    pallas_call x3 -> x2, Pallas kernels: 8.05 us -> 7.45 us  [the longest x1 5.53 us: shards(): pl.pallas_call(sections_kernel, in_specs=[hbm()], out_specs=[vmem()] * 2,...]
  transfers between devices with their start and end apart: 5 -> 1, of which waited for: 4 -> 0; matrix products, arithmetic and copies ran while one was open for 0% -> 0% of each run, Pallas kernels for 31% -> 33%
where the time goes in v2:
time: 40 us; the launch traced here: 39.8 us
  Pallas kernels  21.4 us (54%)
  blocking collectives  10.2 us (25%)
  starting transfers between devices  7.34 us (18%)
  between operations  0.72 us (2%)
    pallas_call x1, Pallas kernels, shards(): pl.pallas_call(functools.partial(update_kernel, gain_polynomial(5), (leng...  13 us
    all_gather x1, blocking collectives, shards(): every = lax.all_gather(pack, 'rect', axis=0)  10.2 us
    all_to_all x1, starting transfers between devices, shards(): lax.all_to_all(pieces, 'slab', split_axis=0, concat_axis=0, tiled=True)  7.34 us
    pallas_call x1, Pallas kernels, shards(): pl.pallas_call(sections_kernel, in_specs=[hbm()], out_specs=[vmem()] * 2,...  5.53 us
    pallas_call x1, Pallas kernels, shards(): pl.pallas_call(forces_kernel, in_specs=[smem()] + [vmem()] * 3, out_specs...  1.92 us
    pallas_call x1, Pallas kernels, shards(): pl.pallas_call(planes_kernel, in_specs=[vmem()] * 2, out_specs=vmem(), ou...  1 us
  transfers between devices with their start and end apart: 1, of which 0 were waited for; matrix products, arithmetic and copies ran while one was open for 0% of the time, Pallas kernels for 33%

profile of v2, /device:TPU:1, one launch (start us, length us, event | category | flops | bytes accessed | tf_op | source)
XLA Modules:
  0.0 39.8 jit_solution(3414256024365778872)
XLA Ops:
  0.6 0.0 copy-start
  0.6 0.0 copy-start.3
  0.7 0.0 copy-start.1
  0.7 0.0 copy-start.4
  0.7 5.5 %sections.1 = (bf16[512,256]{1,0:T(8,128)(2,1)S(1)}, bf16[256,384]{1,0:T(8,128)(2,1)S(1)}) custom-call(bf16[512,32,256]{2,1,0:T(8,128)(2,1)} %bitcast.8), custom_call_target="tpu_custom_call" | custom-call | tf_op jit(solution)/shard_map/sections/pallas_call | solution.py:376
  6.2 10.2 %all-gather = bf16[1024,384]{1,0:T(8,128)(2,1)S(1)} all-gather(bf16[256,384]{1,0:T(8,128)(2,1)S(1)} %get-tuple-element.7), channel_id=2, replica_groups=mesh['rect'=4,'slab'=8] {'rect'}, dimensions={0}, use_global_device_ids=true | all-gather | bytes 983040 | tf_op jit(solution)/shard_map/all_gather | solution.py:392
  16.5 0.0 copy-done
  16.5 0.0 copy-done.4
  16.5 1.9 %forces.1 = (bf16[512,256]{1,0:T(8,128)(2,1)S(1)}, bf16[8,32,384]{2,1,0:T(8,128)(2,1)}) custom-call(s32[4]{0:T(128)S(1)} %copy-done.4, bf16[512,256]{1,0:T(8,128)(2,1)S(1)} %get-tuple-element.6.z_ref, bf16[4,256,384]{2,1,0:T(8,128)(2,1)S(1)} %bitcast.6, bf16[512,512]{1,0:T(8,128)(2,1)S(1)} %copy-done), custom_call_target="tpu_custom_call" | custom-call | tf_op jit(solution)/shard_map/forces/pallas_call | solution.py:393
  18.4 7.3 %all-to-all-start = ((bf16[8,32,384]{2,1,0:T(8,128)(2,1)}), bf16[8,32,384]{2,1,0:T(8,128)(2,1)S(1)}, u32[]{:S(2)}, u32[]{:S(2)}) async-start(bf16[8,32,384]{2,1,0:T(8,128)(2,1)} %get-tuple-element.9), calls=%async_computation | async-start | bytes 393216 | tf_op jit(solution)/shard_map/all_to_all | solution.py:405
  25.7 0.0 copy-done.3
  25.7 0.0 copy-done.1
  25.7 0.0 copy-start.2
  25.8 13.0 %update.1 = bf16[512,32,256]{2,1,0:T(8,128)(2,1)} custom-call(bf16[512,32,256]{2,1,0:T(8,128)(2,1)} %bitcast.9, bf16[512,32,256]{2,1,0:T(8,128)(2,1)} %bitcast.10, bf16[512,256]{1,0:T(8,128)(2,1)S(1)} %get-tuple-element.6.z_ref, bf16[512,256]{1,0:T(8,128)(2,1)S(1)} %get-tuple-element.8.near_ref, bf16[768,128]{1,0:T(8,128)(2,1)S(1)} %copy-done.1, ...), custom_call_target="tpu_custom_call" | custom-call | tf_op jit(solution)/shard_map/update/pallas_call | solution.py:408
  38.7 0.0 all-to-all-done
  38.7 0.0 copy-done.2
  38.8 1.0 %planes.1 = f32[384,256]{1,0:T(8,128)} custom-call(bf16[256,384]{1,0:T(8,128)(2,1)S(1)} %bitcast.7, bf16[256,256]{1,0:T(8,128)(2,1)S(1)} %copy-done.2), custom_call_target="tpu_custom_call" | custom-call | tf_op jit(solution)/shard_map/planes/pallas_call | solution.py:425
Async XLA Ops:
  0.6 15.8 %copy-start = (bf16[512,512]{1,0:T(8,128)(2,1)S(1)}, bf16[512,512]{1,0:T(8,128)(2,1)}, u32[]{:S(2)}) copy-start(bf16[512,512]{1,0:T(8,128)(2,1)} %constant.10.clone.table_ref) | copy-start | bytes 1572868
  0.6 25.1 %copy-start.3 = (bf16[128,256]{1,0:T(8,128)(2,1)S(1)}, bf16[128,256]{1,0:T(8,128)(2,1)}, u32[]{:S(2)}) copy-start(bf16[128,256]{1,0:T(8,128)(2,1)} %constant.8.clone.planes_ref) | copy-start | bytes 196612
  0.7 25.1 %copy-start.1 = (bf16[768,128]{1,0:T(8,128)(2,1)S(1)}, bf16[768,128]{1,0:T(8,128)(2,1)}, u32[]{:S(2)}) copy-start(bf16[768,128]{1,0:T(8,128)(2,1)} %constant.9.clone.mix_ref) | copy-start | bytes 589828
  0.7 15.8 %copy-start.4 = (s32[4]{0:T(128)S(1)}, s32[4]{0:T(128)}, u32[]{:S(2)}) copy-start(s32[4]{0:T(128)} %face_ref.1) | copy-start | bytes 52
  18.4 20.3 %all-to-all-start = ((bf16[8,32,384]{2,1,0:T(8,128)(2,1)}), bf16[8,32,384]{2,1,0:T(8,128)(2,1)S(1)}, u32[]{:S(2)}, u32[]{:S(2)}) async-start(bf16[8,32,384]{2,1,0:T(8,128)(2,1)} %get-tuple-element.9), calls=%async_computation | async-start | bytes 393216 | tf_op jit(solution)/shard_map/all_to_all | solution.py:405
  25.7 13.0 %copy-start.2 = (bf16[256,256]{1,0:T(8,128)(2,1)S(1)}, bf16[256,256]{1,0:T(8,128)(2,1)}, u32[]{:S(2)}) copy-start(bf16[256,256]{1,0:T(8,128)(2,1)} %constant.11.clone.table_ref) | copy-start | bytes 393220

commit v3 on v2

--- a/solution.py
+++ b/solution.py
@@ -17,6 +17,9 @@
 LANES = 128
 GROUP = 16
 USED = PLANES * GROUP
+UNROLL = 2
+SECTION_CHUNKS = 4
+DIRECT = ()
 
 
 def cosine_table(length):
@@ -135,8 +138,7 @@
     row_of_lane = lax.broadcasted_iota(jnp.int32, (8, LANES), 1) % GROUP
     lane = lax.broadcasted_iota(jnp.int32, (GROUP, LANES), 1)
 
-    def body(step, carry):
-        fetch(step).wait()
+    def step_rows(step):
         halves = [[] for _ in range(count)]
         for part in range(4):
             rows = pl.ds((step * 4 + part) * GROUP, GROUP)
@@ -155,6 +157,13 @@
                 pack_ref[pl.ds(half * packed_rows + step * GROUP, GROUP), tile * LANES : (tile + 1) * LANES] = jnp.where(
                     lane < USED, halves[half][tile], moved
                 ).astype(jnp.bfloat16)
+
+    steps = length // (4 * GROUP)
+
+    def body(chunk, carry):
+        fetch(chunk).wait()
+        for step in range(steps):
+            step_rows(chunk * steps + step)
         return carry
 
     lax.fori_loop(0, chunks, body, 0)
@@ -168,18 +177,27 @@
     return partner, source
 
 
-def forces_kernel(face_ref, z_ref, every_ref, table_ref, near_ref, piece_ref):
+def forces_kernel(face_ref, z_ref, *refs):
+    *every_refs, table_ref, near_ref, piece_ref = refs
     count = z_ref.shape[1] // LANES
-    partner, source = neighbours(face_ref, lax.axis_index("rect"))
-    packed_rows = every_ref.shape[1] // count
-    lower = packed_lower_mask((packed_rows, every_ref.shape[2]))
+    rect = lax.axis_index("rect")
+    partner, source = neighbours(face_ref, rect)
+    packed_rows = every_refs[0].shape[-2] // count
+    lower = packed_lower_mask((packed_rows, every_refs[0].shape[-1]))
+
+    def pack_of(other, rows):
+        if len(every_refs) == 1:
+            return every_refs[0][other, rows].astype(jnp.float32)
+        value = every_refs[0][rows].astype(jnp.float32)
+        for distance, ref in enumerate(every_refs[1:], 1):
+            value = jnp.where(other == (rect ^ distance), ref[rows].astype(jnp.float32), value)
+        return value
+
     blocks = packed_rows // GROUP
     lane = lax.broadcasted_iota(jnp.int32, (blocks, GROUP, LANES), 2)
     for half in range(count):
         rows = pl.ds(half * packed_rows, packed_rows)
-        packed = jnp.where(
-            lower, every_ref[partner, rows].astype(jnp.float32), every_ref[source, rows].astype(jnp.float32)
-        )
+        packed = jnp.where(lower, pack_of(partner, rows), pack_of(source, rows))
         tiles = [
             packed[:, tile * LANES : (tile + 1) * LANES].reshape(blocks, GROUP, LANES) for tile in range(3)
         ]
@@ -195,17 +213,18 @@
             for block in range(blocks):
                 start = (block * 4 + group) * GROUP
                 near_ref[start : start + GROUP, half * LANES : (half + 1) * LANES] = value[block]
-    table = table_ref[...]
-
-    def transform(ref, half):
-        modes = ref[:, half * LANES : half * LANES + USED]
-        out = lax.dot_general(modes, table, (((0,), (0,)), ((), ())), preferred_element_type=jnp.float32)
-        out = out.astype(jnp.bfloat16).astype(jnp.float32)
-        return [out[plane * GROUP : (plane + 1) * GROUP] for plane in range(PLANES)]
+    modes = jnp.concatenate([z_ref[...], near_ref[...]], axis=1)
+    cells = lax.dot_general(
+        modes, table_ref[...], (((0,), (0,)), ((), ())), preferred_element_type=jnp.float32
+    )
+    cells = cells.astype(jnp.bfloat16).astype(jnp.float32)
+
+    def sections_of(tile):
+        return [cells[tile * LANES + p * GROUP : tile * LANES + (p + 1) * GROUP] for p in range(PLANES)]
 
     for half in range(count):
-        own = transform(z_ref, half)
-        near = transform(near_ref, half)
+        own = sections_of(half)
+        near = sections_of(count + half)
         jump_up = [near[k] - own[5 - k] for k in range(3)]
         jump_down = [near[5 - k] - own[k] for k in range(3)]
         force = [None] * PLANES
@@ -325,7 +344,7 @@
             advance(group + 1, force_b)
             return inner
 
-        lax.fori_loop(0, pairs, pair, 0)
+        lax.fori_loop(0, pairs, pair, 0, unroll=UNROLL)
         send(chunk).start()
         return carry
 
@@ -372,7 +391,7 @@
     table_x = jnp.asarray(cosine_table(length_x).astype(bf16))
     table_y = jnp.asarray(cosine_table(length_y).astype(bf16))
 
-    chunks = 16
+    chunks = 8
     z_own, pack = pl.pallas_call(
         sections_kernel,
         in_specs=[hbm()],
@@ -383,16 +402,23 @@
         ],
         scratch_shapes=[
             pltpu.VMEM((length_x, local_y, depth_z), bf),
-            pltpu.SemaphoreType.DMA((length_x // (4 * GROUP),)),
+            pltpu.SemaphoreType.DMA((SECTION_CHUNKS,)),
         ],
         compiler_params=limit(16),
         name="sections",
     )(current)
 
-    every = lax.all_gather(pack, "rect", axis=0)
+    rect_count = lax.axis_size("rect")
+    if rect_count in DIRECT:
+        every = [pack]
+        for distance in range(1, rect_count):
+            pairs = [(j, j ^ distance) for j in range(rect_count)]
+            every.append(lax.ppermute(pack, "rect", pairs))
+    else:
+        every = [lax.all_gather(pack, "rect", axis=0)]
     near, pieces = pl.pallas_call(
         forces_kernel,
-        in_specs=[smem()] + [vmem()] * 3,
+        in_specs=[smem()] + [vmem()] * (2 + len(every)),
         out_specs=[vmem()] * 2,
         out_shape=[
             jax.ShapeDtypeStruct((length_x, count * LANES), bf),
@@ -400,7 +426,7 @@
         ],
         compiler_params=limit(8),
         name="forces",
-    )(face_partner, z_own, every, table_x)
+    )(face_partner, z_own, *every, table_x)
 
     arrived = lax.all_to_all(pieces, "slab", split_axis=0, concat_axis=0, tiled=True)
 

time: 40 us -> 39.1 us (0.978)
  Pallas kernels: 21.4 us -> 20.6 us
    pallas_call x1, Pallas kernels: 5.53 us -> 4.88 us  [shards(): pl.pallas_call(sections_kernel, in_specs=[hbm()], out_specs=[vmem()] * 2,...]
where the time goes in v3:
time: 39.1 us; the launch traced here: 38.9 us
  Pallas kernels  20.6 us (53%)
  blocking collectives  10.2 us (26%)
  starting transfers between devices  7.34 us (19%)
  between operations  0.72 us (2%)
    pallas_call x1, Pallas kernels, shards(): pl.pallas_call(functools.partial(update_kernel, gain_polynomial(5), (leng...  12.8 us
    all_gather x1, blocking collectives, shards(): every = [lax.all_gather(pack, 'rect', axis=0)]  10.2 us
    all_to_all x1, starting transfers between devices, shards(): lax.all_to_all(pieces, 'slab', split_axis=0, concat_axis=0, tiled=True)  7.34 us
    pallas_call x1, Pallas kernels, shards(): pl.pallas_call(sections_kernel, in_specs=[hbm()], out_specs=[vmem()] * 2,...  4.88 us
    pallas_call x1, Pallas kernels, shards(): pl.pallas_call(forces_kernel, in_specs=[smem()] + [vmem()] * (2 + len(eve...  1.9 us
    pallas_call x1, Pallas kernels, shards(): pl.pallas_call(planes_kernel, in_specs=[vmem()] * 2, out_specs=vmem(), ou...  1 us
  transfers between devices with their start and end apart: 1, of which 0 were waited for; matrix products, arithmetic and copies ran while one was open for 0% of the time, Pallas kernels for 33%

profile of v3, /device:TPU:1, one launch (start us, length us, event | category | flops | bytes accessed | tf_op | source)
XLA Modules:
  0.0 38.9 jit_solution(7951653035456872773)
XLA Ops:
  0.6 0.0 copy-start
  0.6 0.0 copy-start.3
  0.7 0.0 copy-start.1
  0.7 0.0 copy-start.4
  0.7 4.9 %sections.1 = (bf16[512,256]{1,0:T(8,128)(2,1)S(1)}, bf16[256,384]{1,0:T(8,128)(2,1)S(1)}) custom-call(bf16[512,32,256]{2,1,0:T(8,128)(2,1)} %bitcast.8), custom_call_target="tpu_custom_call" | custom-call | tf_op jit(solution)/shard_map/sections/pallas_call | solution.py:395
  5.6 10.2 %all-gather = bf16[1024,384]{1,0:T(8,128)(2,1)S(1)} all-gather(bf16[256,384]{1,0:T(8,128)(2,1)S(1)} %get-tuple-element.7), channel_id=2, replica_groups=mesh['rect'=4,'slab'=8] {'rect'}, dimensions={0}, use_global_device_ids=true | all-gather | bytes 983040 | tf_op jit(solution)/shard_map/all_gather | solution.py:418
  15.8 0.0 copy-done
  15.8 0.0 copy-done.4
  15.8 1.9 %forces.1 = (bf16[512,256]{1,0:T(8,128)(2,1)S(1)}, bf16[8,32,384]{2,1,0:T(8,128)(2,1)}) custom-call(s32[4]{0:T(128)S(1)} %copy-done.4, bf16[512,256]{1,0:T(8,128)(2,1)S(1)} %get-tuple-element.6.z_ref, bf16[4,256,384]{2,1,0:T(8,128)(2,1)S(1)} %bitcast.6, bf16[512,512]{1,0:T(8,128)(2,1)S(1)} %copy-done), custom_call_target="tpu_custom_call" | custom-call | tf_op jit(solution)/shard_map/forces/pallas_call | solution.py:419
  17.7 7.3 %all-to-all-start = ((bf16[8,32,384]{2,1,0:T(8,128)(2,1)}), bf16[8,32,384]{2,1,0:T(8,128)(2,1)S(1)}, u32[]{:S(2)}, u32[]{:S(2)}) async-start(bf16[8,32,384]{2,1,0:T(8,128)(2,1)} %get-tuple-element.9), calls=%async_computation | async-start | bytes 393216 | tf_op jit(solution)/shard_map/all_to_all | solution.py:431
  25.1 0.0 copy-done.3
  25.1 0.0 copy-done.1
  25.1 0.0 copy-start.2
  25.1 12.8 %update.1 = bf16[512,32,256]{2,1,0:T(8,128)(2,1)} custom-call(bf16[512,32,256]{2,1,0:T(8,128)(2,1)} %bitcast.9, bf16[512,32,256]{2,1,0:T(8,128)(2,1)} %bitcast.10, bf16[512,256]{1,0:T(8,128)(2,1)S(1)} %get-tuple-element.6.z_ref, bf16[512,256]{1,0:T(8,128)(2,1)S(1)} %get-tuple-element.8.near_ref, bf16[768,128]{1,0:T(8,128)(2,1)S(1)} %copy-done.1, ...), custom_call_target="tpu_custom_call" | custom-call | tf_op jit(solution)/shard_map/update/pallas_call | solution.py:434
  37.9 0.0 all-to-all-done
  37.9 0.0 copy-done.2
  37.9 1.0 %planes.1 = f32[384,256]{1,0:T(8,128)} custom-call(bf16[256,384]{1,0:T(8,128)(2,1)S(1)} %bitcast.7, bf16[256,256]{1,0:T(8,128)(2,1)S(1)} %copy-done.2), custom_call_target="tpu_custom_call" | custom-call | tf_op jit(solution)/shard_map/planes/pallas_call | solution.py:451
Async XLA Ops:
  0.6 15.2 %copy-start = (bf16[512,512]{1,0:T(8,128)(2,1)S(1)}, bf16[512,512]{1,0:T(8,128)(2,1)}, u32[]{:S(2)}) copy-start(bf16[512,512]{1,0:T(8,128)(2,1)} %constant.10.clone.refs_1_) | copy-start | bytes 1572868
  0.6 24.4 %copy-start.3 = (bf16[128,256]{1,0:T(8,128)(2,1)S(1)}, bf16[128,256]{1,0:T(8,128)(2,1)}, u32[]{:S(2)}) copy-start(bf16[128,256]{1,0:T(8,128)(2,1)} %constant.8.clone.planes_ref) | copy-start | bytes 196612
  0.7 24.4 %copy-start.1 = (bf16[768,128]{1,0:T(8,128)(2,1)S(1)}, bf16[768,128]{1,0:T(8,128)(2,1)}, u32[]{:S(2)}) copy-start(bf16[768,128]{1,0:T(8,128)(2,1)} %constant.9.clone.mix_ref) | copy-start | bytes 589828
  0.7 15.1 %copy-start.4 = (s32[4]{0:T(128)S(1)}, s32[4]{0:T(128)}, u32[]{:S(2)}) copy-start(s32[4]{0:T(128)} %face_ref.1) | copy-start | bytes 52
  17.7 20.2 %all-to-all-start = ((bf16[8,32,384]{2,1,0:T(8,128)(2,1)}), bf16[8,32,384]{2,1,0:T(8,128)(2,1)S(1)}, u32[]{:S(2)}, u32[]{:S(2)}) async-start(bf16[8,32,384]{2,1,0:T(8,128)(2,1)} %get-tuple-element.9), calls=%async_computation | async-start | bytes 393216 | tf_op jit(solution)/shard_map/all_to_all | solution.py:431
  25.1 12.8 %copy-start.2 = (bf16[256,256]{1,0:T(8,128)(2,1)S(1)}, bf16[256,256]{1,0:T(8,128)(2,1)}, u32[]{:S(2)}) copy-start(bf16[256,256]{1,0:T(8,128)(2,1)} %constant.11.clone.table_ref) | copy-start | bytes 393220

commit v4 on v3

--- a/solution.py
+++ b/solution.py
@@ -17,7 +17,6 @@
 LANES = 128
 GROUP = 16
 USED = PLANES * GROUP
-UNROLL = 2
 SECTION_CHUNKS = 4
 DIRECT = ()
 
@@ -121,7 +120,7 @@
     return values[0]
 
 
-def sections_kernel(now_ref, z_ref, pack_ref, now_vmem, arrivals):
+def sections_kernel(now_ref, prev_ref, z_ref, pack_ref, first_now_ref, first_prev_ref, now_vmem, arrivals, extras):
     count = now_ref.shape[1] // GROUP
     packed_rows = now_ref.shape[0] // 4
     chunks = arrivals.shape[0]
@@ -133,6 +132,13 @@
 
     for chunk in range(chunks):
         fetch(chunk).start()
+    first = pl.ds(0, first_now_ref.shape[0])
+    keeps = [
+        pltpu.make_async_copy(now_ref.at[first], first_now_ref, extras.at[0]),
+        pltpu.make_async_copy(prev_ref.at[first], first_prev_ref, extras.at[1]),
+    ]
+    for copy in keeps:
+        copy.start()
     columns = section_columns(now_ref.shape[2])
     sublane = lax.broadcasted_iota(jnp.int32, (8, LANES), 0)
     row_of_lane = lax.broadcasted_iota(jnp.int32, (8, LANES), 1) % GROUP
@@ -167,6 +173,8 @@
         return carry
 
     lax.fori_loop(0, chunks, body, 0)
+    for copy in keeps:
+        copy.wait()
 
 
 def neighbours(face_ref, rect):
@@ -244,10 +252,10 @@
             )
 
 
-def update_kernel(poly, sides, now_ref, prev_ref, z_ref, near_ref, mix_ref, planes_ref, out_ref, *scratch):
+def update_kernel(poly, sides, now_ref, prev_ref, first_now_ref, first_prev_ref, z_ref, near_ref, mix_ref, planes_ref, out_ref, *scratch):
     now_vmem, prev_vmem, out_vmem, force_a, force_b, modes_ref, square_ref, arrivals, departures = scratch
     length_x, local_y, depth_z = now_vmem.shape
-    chunks = departures.shape[0]
+    chunks = arrivals.shape[1]
     length = length_x // chunks
 
     def rows_of(chunk):
@@ -260,11 +268,13 @@
             pltpu.make_async_copy(prev_ref.at[rows], prev_vmem.at[rows], arrivals.at[1, chunk]),
         ]
 
-    def send(chunk):
-        rows = rows_of(chunk)
-        return pltpu.make_async_copy(out_vmem.at[rows], out_ref.at[rows], departures.at[chunk])
-
-    for chunk in range(chunks):
+    pieces = departures.shape[0] // chunks
+
+    def send(piece):
+        rows = pl.ds(piece * (length // pieces), length // pieces)
+        return pltpu.make_async_copy(out_vmem.at[rows], out_ref.at[rows], departures.at[piece])
+
+    for chunk in range(1, chunks):
         for copy in fetch(chunk):
             copy.start()
     mask = row_mask()[None]
@@ -306,7 +316,7 @@
     reach = middle - 1.0
     begin, after = -middle / reach, (1.0 - middle) / reach
 
-    def advance(group, force_ref):
+    def advance(group, force_ref, now_vmem, prev_vmem):
         row = group * GROUP
         first = row.astype(jnp.float32)
         nodes = [x_square(first + (middle + offset)) for offset in (-reach, 0.0, reach)]
@@ -332,25 +342,26 @@
     make_force(0, force_a)
     pairs = length // (2 * GROUP)
 
+    def compute(chunk, now_rows, prev_rows):
+        for index in range(pairs):
+            group = (chunk * pairs + index) * 2
+            make_force(group + 1, force_b)
+            advance(group, force_a, now_rows, prev_rows)
+            make_force(group + 2, force_a)
+            advance(group + 1, force_b, now_rows, prev_rows)
+            if (index + 1) * pieces % pairs == 0:
+                send(chunk * pieces + (index + 1) * pieces // pairs - 1).start()
+
     def whole(chunk, carry):
         for copy in fetch(chunk):
             copy.wait()
-
-        def pair(index, inner):
-            group = (chunk * pairs + index) * 2
-            make_force(group + 1, force_b)
-            advance(group, force_a)
-            make_force(group + 2, force_a)
-            advance(group + 1, force_b)
-            return inner
-
-        lax.fori_loop(0, pairs, pair, 0, unroll=UNROLL)
-        send(chunk).start()
+        compute(chunk, now_vmem, prev_vmem)
         return carry
 
-    lax.fori_loop(0, chunks, whole, 0)
-    for chunk in range(chunks):
-        send(chunk).wait()
+    compute(jnp.int32(0), first_now_ref, first_prev_ref)
+    lax.fori_loop(1, chunks, whole, 0)
+    for piece in range(pieces * chunks):
+        send(piece).wait()
 
 
 def planes_kernel(arrived_ref, table_ref, out_ref):
@@ -392,21 +403,25 @@
     table_y = jnp.asarray(cosine_table(length_y).astype(bf16))
 
     chunks = 8
-    z_own, pack = pl.pallas_call(
+    first_rows = jax.ShapeDtypeStruct((length_x // chunks, local_y, depth_z), bf)
+    z_own, pack, first_now, first_prev = pl.pallas_call(
         sections_kernel,
-        in_specs=[hbm()],
-        out_specs=[vmem()] * 2,
+        in_specs=[hbm()] * 2,
+        out_specs=[vmem()] * 4,
         out_shape=[
             jax.ShapeDtypeStruct((length_x, count * LANES), bf),
             jax.ShapeDtypeStruct((count * length_x // 4, 3 * LANES), bf),
+            first_rows,
+            first_rows,
         ],
         scratch_shapes=[
             pltpu.VMEM((length_x, local_y, depth_z), bf),
             pltpu.SemaphoreType.DMA((SECTION_CHUNKS,)),
+            pltpu.SemaphoreType.DMA((2,)),
         ],
         compiler_params=limit(16),
         name="sections",
-    )(current)
+    )(current, earlier)
 
     rect_count = lax.axis_size("rect")
     if rect_count in DIRECT:
@@ -433,7 +448,7 @@
     wide = (length_x, local_y, depth_z)
     fresh = pl.pallas_call(
         functools.partial(update_kernel, gain_polynomial(5), (length_x, length_y, depth_z)),
-        in_specs=[hbm(), hbm()] + [vmem()] * 4,
+        in_specs=[hbm(), hbm()] + [vmem()] * 6,
         out_specs=hbm(),
         out_shape=jax.ShapeDtypeStruct(wide, bf),
         scratch_shapes=[
@@ -442,11 +457,11 @@
             pltpu.VMEM((length_x, count * LANES), jnp.float32),
             pltpu.VMEM((local_y, depth_z), jnp.float32),
             pltpu.SemaphoreType.DMA((2, chunks)),
-            pltpu.SemaphoreType.DMA((chunks,)),
+            pltpu.SemaphoreType.DMA((2 * chunks,)),
         ],
         compiler_params=limit(40),
         name="update",
-    )(current, earlier, z_own, near, mix, planes)
+    )(current, earlier, first_now, first_prev, z_own, near, mix, planes)
 
     forcing = pl.pallas_call(
         planes_kernel,

time: 39.1 us -> 37.9 us (0.969)
  Pallas kernels: 20.6 us -> 19.4 us
    pallas_call x1, Pallas kernels: 12.8 us -> 11.5 us  [shards(): pl.pallas_call(functools.partial(update_kernel, gain_polynomial(5), (leng...]
  transfers between devices with their start and end apart: 1 -> 1, of which waited for: 0 -> 0; matrix products, arithmetic and copies ran while one was open for 0% -> 0% of each run, Pallas kernels for 33% -> 30%
where the time goes in v4:
time: 37.9 us; the launch traced here: 37.7 us
  Pallas kernels  19.4 us (51%)
  blocking collectives  10.2 us (27%)
  starting transfers between devices  7.34 us (19%)
  between operations  0.72 us (2%)
    pallas_call x1, Pallas kernels, shards(): pl.pallas_call(functools.partial(update_kernel, gain_polynomial(5), (leng...  11.5 us
    all_gather x1, blocking collectives, shards(): every = [lax.all_gather(pack, 'rect', axis=0)]  10.2 us
    all_to_all x1, starting transfers between devices, shards(): lax.all_to_all(pieces, 'slab', split_axis=0, concat_axis=0, tiled=True)  7.34 us
    pallas_call x1, Pallas kernels, shards(): pl.pallas_call(sections_kernel, in_specs=[hbm()] * 2, out_specs=[vmem()]...  4.98 us
    pallas_call x1, Pallas kernels, shards(): pl.pallas_call(forces_kernel, in_specs=[smem()] + [vmem()] * (2 + len(eve...  1.9 us
    pallas_call x1, Pallas kernels, shards(): pl.pallas_call(planes_kernel, in_specs=[vmem()] * 2, out_specs=vmem(), ou...  1 us
  transfers between devices with their start and end apart: 1, of which 0 were waited for; matrix products, arithmetic and copies ran while one was open for 0% of the time, Pallas kernels for 30%

profile of v4, /device:TPU:1, one launch (start us, length us, event | category | flops | bytes accessed | tf_op | source)
XLA Modules:
  0.0 37.7 jit_solution(17629437234447255207)
XLA Ops:
  0.6 0.0 copy-start
  0.6 0.0 copy-start.4
  0.7 0.0 copy-start.1
  0.7 0.0 copy-start.3
  0.7 5.0 %sections.1 = (bf16[512,256]{1,0:T(8,128)(2,1)S(1)}, bf16[256,384]{1,0:T(8,128)(2,1)S(1)}, bf16[64,32,256]{2,1,0:T(8,128)(2,1)S(1)}, bf16[64,32,256]{2,1,0:T(8,128)(2,1)S(1)}) custom-call(bf16[512,32,256]{2,1,0:T(8,128)(2,1)} %bitcast.8, bf16[512,32,256]{2,1,0:T(8,128)(2,1)} %bitcast.10), custom_call_target="tpu_custom_call" | custom-call | tf_op jit(solution)/shard_map/sections/pallas_call | solution.py:407
  5.7 10.2 %all-gather = bf16[1024,384]{1,0:T(8,128)(2,1)S(1)} all-gather(bf16[256,384]{1,0:T(8,128)(2,1)S(1)} %get-tuple-element.11), channel_id=2, replica_groups=mesh['rect'=4,'slab'=8] {'rect'}, dimensions={0}, use_global_device_ids=true | all-gather | bytes 983040 | tf_op jit(solution)/shard_map/all_gather | solution.py:433
  15.9 0.0 copy-done
  15.9 0.0 copy-done.4
  15.9 1.9 %forces.1 = (bf16[512,256]{1,0:T(8,128)(2,1)S(1)}, bf16[8,32,384]{2,1,0:T(8,128)(2,1)}) custom-call(s32[4]{0:T(128)S(1)} %copy-done.4, bf16[512,256]{1,0:T(8,128)(2,1)S(1)} %get-tuple-element.10.z_ref, bf16[4,256,384]{2,1,0:T(8,128)(2,1)S(1)} %bitcast.6, bf16[512,512]{1,0:T(8,128)(2,1)S(1)} %copy-done), custom_call_target="tpu_custom_call" | custom-call | tf_op jit(solution)/shard_map/forces/pallas_call | solution.py:434
  17.8 7.3 %all-to-all-start = ((bf16[8,32,384]{2,1,0:T(8,128)(2,1)}), bf16[8,32,384]{2,1,0:T(8,128)(2,1)S(1)}, u32[]{:S(2)}, u32[]{:S(2)}) async-start(bf16[8,32,384]{2,1,0:T(8,128)(2,1)} %get-tuple-element.13), calls=%async_computation | async-start | bytes 393216 | tf_op jit(solution)/shard_map/all_to_all | solution.py:446
  25.2 0.0 copy-done.1
  25.2 0.0 copy-done.3
  25.2 0.0 copy-start.2
  25.2 11.5 %update.1 = bf16[512,32,256]{2,1,0:T(8,128)(2,1)} custom-call(bf16[512,32,256]{2,1,0:T(8,128)(2,1)} %bitcast.9, bf16[512,32,256]{2,1,0:T(8,128)(2,1)} %bitcast.11, bf16[64,32,256]{2,1,0:T(8,128)(2,1)S(1)} %get-tuple-element.8.first_now_ref, bf16[64,32,256]{2,1,0:T(8,128)(2,1)S(1)} %get-tuple-element.9.first_prev_ref, ...), custom_call_target="tpu_custom_call" | custom-call | tf_op jit(solution)/shard_map/update/pallas_call | solution.py:449
  36.7 0.0 all-to-all-done
  36.7 0.0 copy-done.2
  36.7 1.0 %planes.1 = f32[384,256]{1,0:T(8,128)} custom-call(bf16[256,384]{1,0:T(8,128)(2,1)S(1)} %bitcast.7, bf16[256,256]{1,0:T(8,128)(2,1)S(1)} %copy-done.2), custom_call_target="tpu_custom_call" | custom-call | tf_op jit(solution)/shard_map/planes/pallas_call | solution.py:466
Async XLA Ops:
  0.6 15.3 %copy-start = (bf16[512,512]{1,0:T(8,128)(2,1)S(1)}, bf16[512,512]{1,0:T(8,128)(2,1)}, u32[]{:S(2)}) copy-start(bf16[512,512]{1,0:T(8,128)(2,1)} %constant.10.clone.refs_1_) | copy-start | bytes 1572868
  0.6 15.3 %copy-start.4 = (s32[4]{0:T(128)S(1)}, s32[4]{0:T(128)}, u32[]{:S(2)}) copy-start(s32[4]{0:T(128)} %face_ref.1) | copy-start | bytes 52
  0.7 24.5 %copy-start.1 = (bf16[768,128]{1,0:T(8,128)(2,1)S(1)}, bf16[768,128]{1,0:T(8,128)(2,1)}, u32[]{:S(2)}) copy-start(bf16[768,128]{1,0:T(8,128)(2,1)} %constant.9.clone.mix_ref) | copy-start | bytes 589828
  0.7 24.5 %copy-start.3 = (bf16[128,256]{1,0:T(8,128)(2,1)S(1)}, bf16[128,256]{1,0:T(8,128)(2,1)}, u32[]{:S(2)}) copy-start(bf16[128,256]{1,0:T(8,128)(2,1)} %constant.8.clone.planes_ref) | copy-start | bytes 196612
  17.8 18.9 %all-to-all-start = ((bf16[8,32,384]{2,1,0:T(8,128)(2,1)}), bf16[8,32,384]{2,1,0:T(8,128)(2,1)S(1)}, u32[]{:S(2)}, u32[]{:S(2)}) async-start(bf16[8,32,384]{2,1,0:T(8,128)(2,1)} %get-tuple-element.13), calls=%async_computation | async-start | bytes 393216 | tf_op jit(solution)/shard_map/all_to_all | solution.py:446
  25.2 11.5 %copy-start.2 = (bf16[256,256]{1,0:T(8,128)(2,1)S(1)}, bf16[256,256]{1,0:T(8,128)(2,1)}, u32[]{:S(2)}) copy-start(bf16[256,256]{1,0:T(8,128)(2,1)} %constant.11.clone.table_ref) | copy-start | bytes 393220

commit v5 on v4

--- a/solution.py
+++ b/solution.py
@@ -350,7 +350,7 @@
             make_force(group + 2, force_a)
             advance(group + 1, force_b, now_rows, prev_rows)
             if (index + 1) * pieces % pairs == 0:
-                send(chunk * pieces + (index + 1) * pieces // pairs - 1).start()
+                send(chunk * pieces + (index + 1) * pieces // pairs - 1).start(priority=1)
 
     def whole(chunk, carry):
         for copy in fetch(chunk):

time: 37.9 us -> 37.9 us (level)
  no operation moved by 1% of the time
where the time goes in v5:
time: 37.9 us; the launch traced here: 37.7 us
  Pallas kernels  19.4 us (51%)
  blocking collectives  10.2 us (27%)
  starting transfers between devices  7.34 us (19%)
  between operations  0.72 us (2%)
    pallas_call x1, Pallas kernels, shards(): pl.pallas_call(functools.partial(update_kernel, gain_polynomial(5), (leng...  11.5 us
    all_gather x1, blocking collectives, shards(): every = [lax.all_gather(pack, 'rect', axis=0)]  10.2 us
    all_to_all x1, starting transfers between devices, shards(): lax.all_to_all(pieces, 'slab', split_axis=0, concat_axis=0, tiled=True)  7.34 us
    pallas_call x1, Pallas kernels, shards(): pl.pallas_call(sections_kernel, in_specs=[hbm()] * 2, out_specs=[vmem()]...  4.98 us
    pallas_call x1, Pallas kernels, shards(): pl.pallas_call(forces_kernel, in_specs=[smem()] + [vmem()] * (2 + len(eve...  1.9 us
    pallas_call x1, Pallas kernels, shards(): pl.pallas_call(planes_kernel, in_specs=[vmem()] * 2, out_specs=vmem(), ou...  1 us
  transfers between devices with their start and end apart: 1, of which 0 were waited for; matrix products, arithmetic and copies ran while one was open for 0% of the time, Pallas kernels for 30%

profile of v5, /device:TPU:1, one launch (start us, length us, event | category | flops | bytes accessed | tf_op | source)
XLA Modules:
  0.0 37.7 jit_solution(342722804693963811)
XLA Ops:
  0.6 0.0 copy-start
  0.6 0.0 copy-start.4
  0.7 0.0 copy-start.1
  0.7 0.0 copy-start.3
  0.7 5.0 %sections.1 = (bf16[512,256]{1,0:T(8,128)(2,1)S(1)}, bf16[256,384]{1,0:T(8,128)(2,1)S(1)}, bf16[64,32,256]{2,1,0:T(8,128)(2,1)S(1)}, bf16[64,32,256]{2,1,0:T(8,128)(2,1)S(1)}) custom-call(bf16[512,32,256]{2,1,0:T(8,128)(2,1)} %bitcast.8, bf16[512,32,256]{2,1,0:T(8,128)(2,1)} %bitcast.10), custom_call_target="tpu_custom_call" | custom-call | tf_op jit(solution)/shard_map/sections/pallas_call | solution.py:407
  5.7 10.2 %all-gather = bf16[1024,384]{1,0:T(8,128)(2,1)S(1)} all-gather(bf16[256,384]{1,0:T(8,128)(2,1)S(1)} %get-tuple-element.11), channel_id=2, replica_groups=mesh['rect'=4,'slab'=8] {'rect'}, dimensions={0}, use_global_device_ids=true | all-gather | bytes 983040 | tf_op jit(solution)/shard_map/all_gather | solution.py:433
  15.9 0.0 copy-done
  15.9 0.0 copy-done.4
  15.9 1.9 %forces.1 = (bf16[512,256]{1,0:T(8,128)(2,1)S(1)}, bf16[8,32,384]{2,1,0:T(8,128)(2,1)}) custom-call(s32[4]{0:T(128)S(1)} %copy-done.4, bf16[512,256]{1,0:T(8,128)(2,1)S(1)} %get-tuple-element.10.z_ref, bf16[4,256,384]{2,1,0:T(8,128)(2,1)S(1)} %bitcast.6, bf16[512,512]{1,0:T(8,128)(2,1)S(1)} %copy-done), custom_call_target="tpu_custom_call" | custom-call | tf_op jit(solution)/shard_map/forces/pallas_call | solution.py:434
  17.8 7.3 %all-to-all-start = ((bf16[8,32,384]{2,1,0:T(8,128)(2,1)}), bf16[8,32,384]{2,1,0:T(8,128)(2,1)S(1)}, u32[]{:S(2)}, u32[]{:S(2)}) async-start(bf16[8,32,384]{2,1,0:T(8,128)(2,1)} %get-tuple-element.13), calls=%async_computation | async-start | bytes 393216 | tf_op jit(solution)/shard_map/all_to_all | solution.py:446
  25.2 0.0 copy-done.1
  25.2 0.0 copy-done.3
  25.2 0.0 copy-start.2
  25.2 11.5 %update.1 = bf16[512,32,256]{2,1,0:T(8,128)(2,1)} custom-call(bf16[512,32,256]{2,1,0:T(8,128)(2,1)} %bitcast.9, bf16[512,32,256]{2,1,0:T(8,128)(2,1)} %bitcast.11, bf16[64,32,256]{2,1,0:T(8,128)(2,1)S(1)} %get-tuple-element.8.first_now_ref, bf16[64,32,256]{2,1,0:T(8,128)(2,1)S(1)} %get-tuple-element.9.first_prev_ref, ...), custom_call_target="tpu_custom_call" | custom-call | tf_op jit(solution)/shard_map/update/pallas_call | solution.py:449
  36.7 0.0 all-to-all-done
  36.7 0.0 copy-done.2
  36.7 1.0 %planes.1 = f32[384,256]{1,0:T(8,128)} custom-call(bf16[256,384]{1,0:T(8,128)(2,1)S(1)} %bitcast.7, bf16[256,256]{1,0:T(8,128)(2,1)S(1)} %copy-done.2), custom_call_target="tpu_custom_call" | custom-call | tf_op jit(solution)/shard_map/planes/pallas_call | solution.py:466
Async XLA Ops:
  0.6 15.3 %copy-start = (bf16[512,512]{1,0:T(8,128)(2,1)S(1)}, bf16[512,512]{1,0:T(8,128)(2,1)}, u32[]{:S(2)}) copy-start(bf16[512,512]{1,0:T(8,128)(2,1)} %constant.10.clone.refs_1_) | copy-start | bytes 1572868
  0.6 15.3 %copy-start.4 = (s32[4]{0:T(128)S(1)}, s32[4]{0:T(128)}, u32[]{:S(2)}) copy-start(s32[4]{0:T(128)} %face_ref.1) | copy-start | bytes 52
  0.7 24.5 %copy-start.1 = (bf16[768,128]{1,0:T(8,128)(2,1)S(1)}, bf16[768,128]{1,0:T(8,128)(2,1)}, u32[]{:S(2)}) copy-start(bf16[768,128]{1,0:T(8,128)(2,1)} %constant.9.clone.mix_ref) | copy-start | bytes 589828
  0.7 24.5 %copy-start.3 = (bf16[128,256]{1,0:T(8,128)(2,1)S(1)}, bf16[128,256]{1,0:T(8,128)(2,1)}, u32[]{:S(2)}) copy-start(bf16[128,256]{1,0:T(8,128)(2,1)} %constant.8.clone.planes_ref) | copy-start | bytes 196612
  17.8 18.9 %all-to-all-start = ((bf16[8,32,384]{2,1,0:T(8,128)(2,1)}), bf16[8,32,384]{2,1,0:T(8,128)(2,1)S(1)}, u32[]{:S(2)}, u32[]{:S(2)}) async-start(bf16[8,32,384]{2,1,0:T(8,128)(2,1)} %get-tuple-element.13), calls=%async_computation | async-start | bytes 393216 | tf_op jit(solution)/shard_map/all_to_all | solution.py:446
  25.2 11.5 %copy-start.2 = (bf16[256,256]{1,0:T(8,128)(2,1)S(1)}, bf16[256,256]{1,0:T(8,128)(2,1)}, u32[]{:S(2)}) copy-start(bf16[256,256]{1,0:T(8,128)(2,1)} %constant.11.clone.table_ref) | copy-start | bytes 393220

commit v6 on v5

--- a/solution.py
+++ b/solution.py
@@ -186,7 +186,7 @@
 
 
 def forces_kernel(face_ref, z_ref, *refs):
-    *every_refs, table_ref, near_ref, piece_ref = refs
+    *every_refs, table_ref, near_ref, piece_out_ref, piece_ref, departures = refs
     count = z_ref.shape[1] // LANES
     rect = lax.axis_index("rect")
     partner, source = neighbours(face_ref, rect)
@@ -230,6 +230,7 @@
     def sections_of(tile):
         return [cells[tile * LANES + p * GROUP : tile * LANES + (p + 1) * GROUP] for p in range(PLANES)]
 
+    copies = []
     for half in range(count):
         own = sections_of(half)
         near = sections_of(count + half)
@@ -250,6 +251,13 @@
             piece_ref[slot, half * GROUP : (half + 1) * GROUP, :] = jnp.concatenate(parts, axis=1).astype(
                 jnp.bfloat16
             )
+        rows = slice(half * GROUP, (half + 1) * GROUP)
+        copies.append(
+            pltpu.make_async_copy(piece_ref.at[:, rows], piece_out_ref.at[:, rows], departures.at[half])
+        )
+        copies[-1].start()
+    for copy in copies:
+        copy.wait()
 
 
 def update_kernel(poly, sides, now_ref, prev_ref, first_now_ref, first_prev_ref, z_ref, near_ref, mix_ref, planes_ref, out_ref, *scratch):
@@ -364,11 +372,19 @@
         send(piece).wait()
 
 
-def planes_kernel(arrived_ref, table_ref, out_ref):
-    out = lax.dot_general(
-        arrived_ref[...], table_ref[...], (((0,), (0,)), ((), ())), preferred_element_type=jnp.float32
-    )
-    out_ref[...] = out
+def planes_kernel(arrived_ref, table_ref, out_ref, out_vmem, departures):
+    parts = departures.shape[0]
+    length = out_vmem.shape[0] // parts
+    copies = []
+    for part in range(parts):
+        rows = slice(part * length, (part + 1) * length)
+        out_vmem[rows] = lax.dot_general(
+            arrived_ref[:, rows], table_ref[...], (((0,), (0,)), ((), ())), preferred_element_type=jnp.float32
+        )
+        copies.append(pltpu.make_async_copy(out_vmem.at[rows], out_ref.at[rows], departures.at[part]))
+        copies[-1].start()
+    for copy in copies:
+        copy.wait()
 
 
 def smem():
@@ -431,14 +447,16 @@
             every.append(lax.ppermute(pack, "rect", pairs))
     else:
         every = [lax.all_gather(pack, "rect", axis=0)]
+    piece_shape = (slab_count, local_y, PLANES * local_x)
     near, pieces = pl.pallas_call(
         forces_kernel,
         in_specs=[smem()] + [vmem()] * (2 + len(every)),
-        out_specs=[vmem()] * 2,
+        out_specs=[vmem(), hbm()],
         out_shape=[
             jax.ShapeDtypeStruct((length_x, count * LANES), bf),
-            jax.ShapeDtypeStruct((slab_count, local_y, PLANES * local_x), bf),
+            jax.ShapeDtypeStruct(piece_shape, bf),
         ],
+        scratch_shapes=[pltpu.VMEM(piece_shape, bf), pltpu.SemaphoreType.DMA((count,))],
         compiler_params=limit(8),
         name="forces",
     )(face_partner, z_own, *every, table_x)
@@ -463,11 +481,13 @@
         name="update",
     )(current, earlier, first_now, first_prev, z_own, near, mix, planes)
 
+    cells = (PLANES * local_x, length_y)
     forcing = pl.pallas_call(
         planes_kernel,
         in_specs=[vmem()] * 2,
-        out_specs=vmem(),
-        out_shape=jax.ShapeDtypeStruct((PLANES * local_x, length_y), jnp.float32),
+        out_specs=hbm(),
+        out_shape=jax.ShapeDtypeStruct(cells, jnp.float32),
+        scratch_shapes=[pltpu.VMEM(cells, jnp.float32), pltpu.SemaphoreType.DMA((3,))],
         compiler_params=limit(8),
         name="planes",
     )(arrived.reshape(length_y, PLANES * local_x), table_y)

time: 37.9 us -> 37.9 us (level)
  no operation moved by 1% of the time
where the time goes in v6:
time: 37.9 us; the launch traced here: 37.7 us
  Pallas kernels  19.4 us (51%)
  blocking collectives  10.2 us (27%)
  starting transfers between devices  7.35 us (19%)
  between operations  0.72 us (2%)
    pallas_call x1, Pallas kernels, shards(): pl.pallas_call(functools.partial(update_kernel, gain_polynomial(5), (leng...  11.5 us
    all_gather x1, blocking collectives, shards(): every = [lax.all_gather(pack, 'rect', axis=0)]  10.2 us
    all_to_all x1, starting transfers between devices, shards(): lax.all_to_all(pieces, 'slab', split_axis=0, concat_axis=0, tiled=True)  7.35 us
    pallas_call x1, Pallas kernels, shards(): pl.pallas_call(sections_kernel, in_specs=[hbm()] * 2, out_specs=[vmem()]...  4.98 us
    pallas_call x1, Pallas kernels, shards(): pl.pallas_call(forces_kernel, in_specs=[smem()] + [vmem()] * (2 + len(eve...  1.88 us
    pallas_call x1, Pallas kernels, shards(): pl.pallas_call(planes_kernel, in_specs=[vmem()] * 2, out_specs=hbm(), out...  0.99 us
  transfers between devices with their start and end apart: 1, of which 0 were waited for; matrix products, arithmetic and copies ran while one was open for 0% of the time, Pallas kernels for 30%

profile of v6, /device:TPU:1, one launch (start us, length us, event | category | flops | bytes accessed | tf_op | source)
XLA Modules:
  0.0 37.7 jit_solution(4714141049016021378)
XLA Ops:
  0.6 0.0 copy-start
  0.6 0.0 copy-start.4
  0.7 0.0 copy-start.1
  0.7 0.0 copy-start.3
  0.7 5.0 %sections.1 = (bf16[512,256]{1,0:T(8,128)(2,1)S(1)}, bf16[256,384]{1,0:T(8,128)(2,1)S(1)}, bf16[64,32,256]{2,1,0:T(8,128)(2,1)S(1)}, bf16[64,32,256]{2,1,0:T(8,128)(2,1)S(1)}) custom-call(bf16[512,32,256]{2,1,0:T(8,128)(2,1)} %bitcast.8, bf16[512,32,256]{2,1,0:T(8,128)(2,1)} %bitcast.10), custom_call_target="tpu_custom_call" | custom-call | tf_op jit(solution)/shard_map/sections/pallas_call | solution.py:423
  5.7 10.2 %all-gather = bf16[1024,384]{1,0:T(8,128)(2,1)S(1)} all-gather(bf16[256,384]{1,0:T(8,128)(2,1)S(1)} %get-tuple-element.11), channel_id=2, replica_groups=mesh['rect'=4,'slab'=8] {'rect'}, dimensions={0}, use_global_device_ids=true | all-gather | bytes 983040 | tf_op jit(solution)/shard_map/all_gather | solution.py:449
  15.9 0.0 copy-done
  15.9 0.0 copy-done.4
  15.9 1.9 %forces.1 = (bf16[512,256]{1,0:T(8,128)(2,1)S(1)}, bf16[8,32,384]{2,1,0:T(8,128)(2,1)}) custom-call(s32[4]{0:T(128)S(1)} %copy-done.4, bf16[512,256]{1,0:T(8,128)(2,1)S(1)} %get-tuple-element.10.z_ref, bf16[4,256,384]{2,1,0:T(8,128)(2,1)S(1)} %bitcast.6, bf16[512,512]{1,0:T(8,128)(2,1)S(1)} %copy-done), custom_call_target="tpu_custom_call" | custom-call | tf_op jit(solution)/shard_map/forces/pallas_call | solution.py:451
  17.8 7.4 %all-to-all-start = ((bf16[8,32,384]{2,1,0:T(8,128)(2,1)}), bf16[8,32,384]{2,1,0:T(8,128)(2,1)S(1)}, u32[]{:S(2)}, u32[]{:S(2)}) async-start(bf16[8,32,384]{2,1,0:T(8,128)(2,1)} %get-tuple-element.13), calls=%async_computation | async-start | bytes 393216 | tf_op jit(solution)/shard_map/all_to_all | solution.py:464
  25.2 0.0 copy-done.1
  25.2 0.0 copy-done.3
  25.2 0.0 copy-start.2
  25.2 11.5 %update.1 = bf16[512,32,256]{2,1,0:T(8,128)(2,1)} custom-call(bf16[512,32,256]{2,1,0:T(8,128)(2,1)} %bitcast.9, bf16[512,32,256]{2,1,0:T(8,128)(2,1)} %bitcast.11, bf16[64,32,256]{2,1,0:T(8,128)(2,1)S(1)} %get-tuple-element.8.first_now_ref, bf16[64,32,256]{2,1,0:T(8,128)(2,1)S(1)} %get-tuple-element.9.first_prev_ref, ...), custom_call_target="tpu_custom_call" | custom-call | tf_op jit(solution)/shard_map/update/pallas_call | solution.py:467
  36.7 0.0 all-to-all-done
  36.7 0.0 copy-done.2
  36.7 1.0 %planes.1 = f32[384,256]{1,0:T(8,128)} custom-call(bf16[256,384]{1,0:T(8,128)(2,1)S(1)} %bitcast.7, bf16[256,256]{1,0:T(8,128)(2,1)S(1)} %copy-done.2), custom_call_target="tpu_custom_call" | custom-call | tf_op jit(solution)/shard_map/planes/pallas_call | solution.py:485
Async XLA Ops:
  0.6 15.3 %copy-start = (bf16[512,512]{1,0:T(8,128)(2,1)S(1)}, bf16[512,512]{1,0:T(8,128)(2,1)}, u32[]{:S(2)}) copy-start(bf16[512,512]{1,0:T(8,128)(2,1)} %constant.10.clone.refs_1_) | copy-start | bytes 1572868
  0.6 15.3 %copy-start.4 = (s32[4]{0:T(128)S(1)}, s32[4]{0:T(128)}, u32[]{:S(2)}) copy-start(s32[4]{0:T(128)} %face_ref.1) | copy-start | bytes 52
  0.7 24.5 %copy-start.1 = (bf16[768,128]{1,0:T(8,128)(2,1)S(1)}, bf16[768,128]{1,0:T(8,128)(2,1)}, u32[]{:S(2)}) copy-start(bf16[768,128]{1,0:T(8,128)(2,1)} %constant.9.clone.mix_ref) | copy-start | bytes 589828
  0.7 24.5 %copy-start.3 = (bf16[128,256]{1,0:T(8,128)(2,1)S(1)}, bf16[128,256]{1,0:T(8,128)(2,1)}, u32[]{:S(2)}) copy-start(bf16[128,256]{1,0:T(8,128)(2,1)} %constant.8.clone.planes_ref) | copy-start | bytes 196612
  17.8 18.9 %all-to-all-start = ((bf16[8,32,384]{2,1,0:T(8,128)(2,1)}), bf16[8,32,384]{2,1,0:T(8,128)(2,1)S(1)}, u32[]{:S(2)}, u32[]{:S(2)}) async-start(bf16[8,32,384]{2,1,0:T(8,128)(2,1)} %get-tuple-element.13), calls=%async_computation | async-start | bytes 393216 | tf_op jit(solution)/shard_map/all_to_all | solution.py:464
  25.2 11.5 %copy-start.2 = (bf16[256,256]{1,0:T(8,128)(2,1)S(1)}, bf16[256,256]{1,0:T(8,128)(2,1)}, u32[]{:S(2)}) copy-start(bf16[256,256]{1,0:T(8,128)(2,1)} %constant.11.clone.table_ref) | copy-start | bytes 393220
